TPU v7x, 128 devices: a whole 4x4x4 slice. The times are simulated.
128 devices in a mesh: chan: 16 (over y, x), stn: 8 (over z, core).
Axes of the slice: x: 4, y: 4, z: 4, core: 2. Of those that a mesh axis runs over, the one named last changes fastest.
Arguments:
- measured_correlation: float32 [16, 8, 8192], P('chan', None, 'stn'), may hold values from -3 to 3
- model_correlation: float32 [16, 8, 16, 8192], P('chan', None, None, 'stn'), may hold values from -0.75 to 0.75
- source_pointing: int32 [16, 1], replicated, may hold values from 0 to 7
- antenna_pairs: int32 [2, 8192], P(None, 'stn'), may hold values from 0 to 511, as said below
- starting_jones_matrices: float32 [16, 8, 8, 512], P('chan'), may hold values from -1 to 2
- starting_polynomial_terms: float32 [3, 8, 8, 512], replicated, may hold values from -1 to 2
- starting_lagrange_scaled: float32 [16, 8, 8, 512], P('chan'), may hold values from -1.5 to 1.5
- augmented_lagrange_rhos: float32 [8], replicated, may hold values from 0.5 to 4
Outputs:
- solved_gains: float32 [16, 8, 8, 512], P('chan', None, None, 'stn')
- solved_dual: float32 [16, 8, 8, 512], P('chan', None, None, 'stn')
- fit_coeffs: float32 [3, 8, 8, 512], P(None, None, None, 'stn')
Inputs may be any that keep to these rules, and one draw needn't show every extreme that they name: `antenna_pairs`: row 0 holds a baseline's first station and row 1 its second, which differs from the first. The first station of every baseline in the i-th aligned block of 1024 baselines lies among stations i * 64 to (i + 1) * 64 - 1. `source_pointing`: every direction holds at least one component.
All inputs are finite; a program needn't handle non-finite values.
Results may differ from a plain program's by a relative error of at most 0.0001.
Values sent between devices are 32-bit elements; how exact they have to be, the bound alone decides.
A program may use at most 64 MiB of HBM per device.

v0:
```python
from functools import partial

import jax
import jax.numpy as jnp
from jax import lax
from jax.sharding import Mesh
from jax.sharding import PartitionSpec as P

CALIB_PATHS = 8
TERMS = 3
STEPS = 2
INNER = 2
STN = ("stn_0", "stn_1")
CHAN = ("chan_0", "chan_1")
CHAN_STN = ("chan_0", "chan_1", "stn_0", "stn_1")


student_nu = 2.0
squared_tolerance = 1e-06
highest = lax.Precision.HIGHEST


def over_axes(value, axes):
    for axis in axes:
        value = lax.psum(value, axis)
    return value


def split_up(value, dim, length):
    before, after = (value.shape[:dim], value.shape[dim + 1 :])
    return jnp.moveaxis(value.reshape(*before, length, -1, *after), dim, 0)


def sent_and_summed(value, axis, dim):
    length = lax.axis_size(axis)
    blocks = lax.all_to_all(split_up(value, dim, length), axis, 0, 0, tiled=True)
    return jnp.sum(blocks, axis=0)


def copy_for_each(value, axis):
    length = lax.axis_size(axis)
    return lax.all_to_all(
        jnp.broadcast_to(value[None], (length, *value.shape)), axis, 0, 0, tiled=True
    )


def laid_out(blocks, dim):
    blocks = jnp.moveaxis(blocks, 0, dim)
    shape = blocks.shape
    return blocks.reshape(*shape[:dim], shape[dim] * shape[dim + 1], *shape[dim + 2 :])


def gathered_copies(value, axis, dim):
    blocks = copy_for_each(value, axis)
    return laid_out(blocks, dim)


def over_pieces(value, axis):
    return lax.all_gather(value, axis).sum(0)


def entries(stacked):
    return [(stacked[slot_idx], stacked[4 + slot_idx]) for slot_idx in range(4)]


def assemble(matrix):
    return jnp.stack(
        [matrix[slot_idx][0] for slot_idx in range(4)]
        + [matrix[slot_idx][1] for slot_idx in range(4)],
        axis=0,
    )


def flatten(matrix):
    return [matrix[slot_idx][0] for slot_idx in range(4)] + [
        matrix[slot_idx][1] for slot_idx in range(4)
    ]


def multiply_pair(first_pair, second_pair):
    return (
        first_pair[0] * second_pair[0] - first_pair[1] * second_pair[1],
        first_pair[0] * second_pair[1] + first_pair[1] * second_pair[0],
    )


def add_pair(first_pair, second_pair):
    return (first_pair[0] + second_pair[0], first_pair[1] + second_pair[1])


def conjugate(value_pair):
    return (value_pair[0], -value_pair[1])


def matrix_product(factor_one, factor_two):
    return [
        add_pair(
            multiply_pair(factor_one[0], factor_two[0]), multiply_pair(factor_one[1], factor_two[2])
        ),
        add_pair(
            multiply_pair(factor_one[0], factor_two[1]), multiply_pair(factor_one[1], factor_two[3])
        ),
        add_pair(
            multiply_pair(factor_one[2], factor_two[0]), multiply_pair(factor_one[3], factor_two[2])
        ),
        add_pair(
            multiply_pair(factor_one[2], factor_two[1]), multiply_pair(factor_one[3], factor_two[3])
        ),
    ]


def adjoint(matrix):
    return [conjugate(matrix[0]), conjugate(matrix[2]), conjugate(matrix[1]), conjugate(matrix[3])]


def gram_parts(matrix):
    upper_sum = (
        matrix[0][0] * matrix[0][0]
        + matrix[0][1] * matrix[0][1]
        + matrix[1][0] * matrix[1][0]
        + matrix[1][1] * matrix[1][1]
    )
    lower_sum = (
        matrix[2][0] * matrix[2][0]
        + matrix[2][1] * matrix[2][1]
        + matrix[3][0] * matrix[3][0]
        + matrix[3][1] * matrix[3][1]
    )
    cross_term = add_pair(
        multiply_pair(matrix[0], conjugate(matrix[2])),
        multiply_pair(matrix[1], conjugate(matrix[3])),
    )
    return [upper_sum, lower_sum, cross_term[0], cross_term[1]]


def basis_table(channel_count):
    frequency = (2.0 * jnp.arange(channel_count, dtype=jnp.float32) + 1.0) / channel_count - 1.0
    columns = []
    for degree in range(TERMS):
        column = frequency**degree
        for earlier in columns:
            column = column - jnp.sum(earlier * column) / channel_count * earlier
        column = column / jnp.sqrt(jnp.sum(column * column) / channel_count)
        columns.append(column)
    return jnp.stack(columns, axis=1)


def combine_sources(cohere_f, source_pointing):
    member = (
        source_pointing[:, 0][:, None] == jnp.arange(CALIB_PATHS, dtype=jnp.int32)[None, :]
    ).astype(jnp.float32)
    return jnp.einsum("csb,sk->ckb", cohere_f, member, precision=highest)


def channel_state(vis_f, cohere_dir, spectral_jones_matrices, antenna_pairs):
    coherent = entries(cohere_dir)
    first_gain = entries(spectral_jones_matrices[:, :, antenna_pairs[0]])
    second_gain = entries(spectral_jones_matrices[:, :, antenna_pairs[1]])
    toward_first = matrix_product(coherent, adjoint(second_gain))
    own_terms = matrix_product(first_gain, toward_first)
    observed = entries(vis_f)
    residual = [
        (
            observed[slot_idx][0] - jnp.sum(own_terms[slot_idx][0], axis=0),
            observed[slot_idx][1] - jnp.sum(own_terms[slot_idx][1], axis=0),
        )
        for slot_idx in range(4)
    ]
    energy = residual[0][0] * residual[0][0] + residual[0][1] * residual[0][1]
    for slot_idx in range(1, 4):
        energy = (
            energy
            + residual[slot_idx][0] * residual[slot_idx][0]
            + residual[slot_idx][1] * residual[slot_idx][1]
        )
    return (residual, own_terms, toward_first, first_gain, coherent, energy)


def channel_sums(chan_state, weight, first_table, second_table, block_start):
    residual, own_terms, toward_first, first_gain, coherent, energy = chan_state
    target = [
        add_pair((residual[slot_idx][0][None], residual[slot_idx][1][None]), own_terms[slot_idx])
        for slot_idx in range(4)
    ]
    back_terms = matrix_product(first_gain, coherent)
    first_parts = (
        jnp.stack(
            gram_parts(toward_first) + flatten(matrix_product(target, adjoint(toward_first))),
            axis=0,
        )
        * weight
    )
    second_parts = (
        jnp.stack(
            gram_parts(adjoint(back_terms)) + flatten(matrix_product(adjoint(target), back_terms)),
            axis=0,
        )
        * weight
    )
    first_block = jnp.einsum("pkb,bs->pks", first_parts, first_table, precision=highest)
    every_station = jnp.einsum("pkb,bs->pks", second_parts, second_table, precision=highest)
    block_width = first_table.shape[1]
    own_rows = lax.dynamic_slice_in_dim(every_station, block_start, block_width, 2) + first_block
    return lax.dynamic_update_slice_in_dim(every_station, own_rows, block_start, 2)


def jones_estimator(
    least_squares_equations, pivot_spectral_point, spectral_jones_matrices, augmented_lagrange_rhos
):
    augmented_rho_factor = augmented_lagrange_rhos[:, None]
    diag_one = least_squares_equations[0] + augmented_rho_factor
    diag_two = least_squares_equations[1] + augmented_rho_factor
    determinant = (
        diag_one * diag_two
        - least_squares_equations[2] * least_squares_equations[2]
        - least_squares_equations[3] * least_squares_equations[3]
    )
    zero_part = jnp.zeros_like(determinant)
    inverse = [
        (diag_two / determinant, zero_part),
        (-least_squares_equations[2] / determinant, -least_squares_equations[3] / determinant),
        (-least_squares_equations[2] / determinant, least_squares_equations[3] / determinant),
        (diag_one / determinant, zero_part),
    ]
    right_side = entries(
        least_squares_equations[4:] + augmented_rho_factor[None] * pivot_spectral_point
    )
    solution = assemble(matrix_product(right_side, inverse))
    return 0.5 * (spectral_jones_matrices + solution)


def body(
    measured_correlation,
    model_correlation,
    source_pointing,
    antenna_pairs,
    starting_jones_matrices,
    starting_polynomial_terms,
    starting_lagrange_scaled,
    augmented_lagrange_rhos,
):
    local_ch = measured_correlation.shape[0]
    stations = starting_jones_matrices.shape[3]
    block_size = stations // lax.axis_size(STN)
    block_start = lax.axis_index(STN) * block_size
    total_ch = local_ch * lax.axis_size(CHAN)
    sample_count = total_ch * measured_correlation.shape[2] * lax.axis_size(STN)
    my_basis = lax.dynamic_slice_in_dim(
        basis_table(total_ch), lax.axis_index(CHAN) * local_ch, local_ch, 0
    )
    cohere_dir = jax.vmap(combine_sources, (0, None))(model_correlation, source_pointing)
    first_table = (
        (antenna_pairs[0] - block_start)[:, None]
        == jnp.arange(block_size, dtype=jnp.int32)[None, :]
    ).astype(jnp.float32)
    second_table = (
        antenna_pairs[1][:, None] == jnp.arange(stations, dtype=jnp.int32)[None, :]
    ).astype(jnp.float32)
    state_fn = jax.vmap(channel_state, (0, 0, 0, None))
    sums_fn = jax.vmap(
        partial(
            channel_sums,
            first_table=first_table,
            second_table=second_table,
            block_start=block_start,
        ),
        (0, 0),
    )
    estimate_routine = jax.vmap(jones_estimator, (0, 0, 0, None))

    def own_block(array):
        return lax.dynamic_slice_in_dim(array, block_start, block_size, 3)

    consensus = jnp.einsum("ft,tcks->fcks", my_basis, starting_polynomial_terms, precision=highest)
    whole_jones_matrix = starting_jones_matrices
    consensus = own_block(consensus)
    dual_now = own_block(starting_lagrange_scaled)
    gain_mine = own_block(starting_jones_matrices)
    pending = None
    fit_now = starting_polynomial_terms
    for step_idx in range(STEPS):
        pivot_antenna = consensus - dual_now
        for inner_idx in range(INNER):
            chan_state = state_fn(
                measured_correlation, cohere_dir, whole_jones_matrix, antenna_pairs
            )
            mean_square = (
                over_axes(jnp.sum(chan_state[5]), CHAN_STN) / sample_count + squared_tolerance
            )
            weight = (student_nu + 2.0) / (student_nu + chan_state[5] / mean_square)
            least_squares_equations = sums_fn(chan_state, weight)
            final_pass = step_idx == STEPS - 1 and inner_idx == INNER - 1
            block_sums = sent_and_summed(least_squares_equations, STN, 3)
            gain_mine = estimate_routine(
                block_sums, pivot_antenna, gain_mine, augmented_lagrange_rhos
            )
            if not final_pass:
                whole_jones_matrix = gathered_copies(gain_mine, STN, 3)
        partial_fit = jnp.einsum("ft,fcks->tcks", my_basis, gain_mine + dual_now, precision=highest)
        fit_now = over_pieces(partial_fit, CHAN) / total_ch
        consensus = jnp.einsum("ft,tcks->fcks", my_basis, fit_now, precision=highest)
        dual_now = dual_now + gain_mine - consensus
    return (gain_mine, dual_now, fit_now)


def solution(mesh):
    torus = Mesh(mesh.devices.reshape(4, 4, 4, 2), ("chan_0", "chan_1", "stn_0", "stn_1"))
    placed = (
        P(CHAN, None, STN),
        P(CHAN, None, None, STN),
        P(),
        P(None, STN),
        P(CHAN, None, None, None),
        P(),
        P(CHAN, None, None, None),
        P(),
    )
    return jax.shard_map(
        body,
        mesh=torus,
        in_specs=placed,
        out_specs=(P(CHAN, None, None, STN), P(CHAN, None, None, STN), P(None, None, None, STN)),
        check_vma=False,
    )
```

profile of v0, /device:TPU:1, one launch (start us, length us, event | category | flops | bytes accessed | tf_op | source)
XLA Modules:
  0.0 394.0 jit_solution(17841108396992210272)
XLA Ops:
  4.9 9.1 %gather_fusion.1 = f32[1024,8,8]{2,1,0:T(8,128)} fusion(f32[8,8,512]{1,0,2:T(8,128)S(1)} %bitcast.1080, s32[1024]{0:T(1024)S(1)} %get-tuple-element.366), kind=kCustom, calls=%fused_computation.1 | custom fusion | bytes 528384 | tf_op jit(solution)/shard_map/vmap()/gather | solution.py:158
  14.0 2.8 copy.543
  16.8 9.1 %gather_fusion = f32[1024,8,8]{2,1,0:T(8,128)} fusion(f32[8,8,512]{1,0,2:T(8,128)S(1)} %bitcast.1081, s32[1024]{0:T(1024)S(1)} %get-tuple-element.367), kind=kCustom, calls=%fused_computation | custom fusion | bytes 528384 | tf_op jit(solution)/shard_map/vmap()/gather | solution.py:157
  25.9 2.8 copy.531
  30.0 10.2 %psum.112 = f32[]{:T(128)} all-reduce(f32[]{:T(128)} %fusion.213), channel_id=1, replica_groups=mesh['chan_0'=4,'chan_1'=4,'stn_0'=4,'stn_1'=2] {'chan_0'}, use_global_device_ids=true, to_apply=%region_9.0 | all-reduce | flops 1 | bytes 8 | tf_op jit(solution)/shard_map/psum | solution.py:25
  40.3 9.4 %psum.113 = f32[]{:T(128)} all-reduce(f32[]{:T(128)} %psum.112), channel_id=1, replica_groups=mesh['chan_0'=4,'chan_1'=4,'stn_0'=4,'stn_1'=2] {'chan_1'}, use_global_device_ids=true, to_apply=%region_10.0 | all-reduce | flops 1 | bytes 8 | tf_op jit(solution)/shard_map/psum | solution.py:25
  50.3 10.4 %psum.114 = f32[]{:T(128)} all-reduce(f32[]{:T(128)} %psum.113), channel_id=1, replica_groups=mesh['chan_0'=4,'chan_1'=4,'stn_0'=4,'stn_1'=2] {'stn_0'}, use_global_device_ids=true, to_apply=%region_11.0 | all-reduce | flops 1 | bytes 8 | tf_op jit(solution)/shard_map/psum | solution.py:25
  61.2 9.2 %psum.115 = f32[]{:T(128)} all-reduce(f32[]{:T(128)} %psum.114), channel_id=1, replica_groups=mesh['chan_0'=4,'chan_1'=4,'stn_0'=4,'stn_1'=2] {'stn_1'}, use_global_device_ids=true, to_apply=%region_12.0 | all-reduce | flops 1 | bytes 8 | tf_op jit(solution)/shard_map/psum | solution.py:25
  75.7 2.5 scatter.14
  79.3 3.3 all-to-all-start
  93.0 8.8 %all_to_all.35 = f32[8,1,4096]{2,1,0:T(1,128)S(1)} all-to-all(f32[8,1,4096]{2,1,0:T(1,128)S(1)} %reshape.20802), channel_id=1, replica_groups=mesh['chan_0'=4,'chan_1'=4,'stn_0'=4,'stn_1'=2] {'stn_0','stn_1'}, dimensions={0} | all-to-all | bytes 262144 | tf_op jit(solution)/shard_map/all_to_all | solution.py:42
  103.6 9.1 %gather_fusion.3 = f32[1024,8,8]{2,1,0:T(8,128)} fusion(f32[8,8,512]{1,0,2:T(8,128)S(1)} %bitcast.1084, s32[1024]{0:T(1024)S(1)} %get-tuple-element.366), kind=kCustom, calls=%fused_computation.3 | custom fusion | bytes 528384 | tf_op jit(solution)/shard_map/vmap()/gather | solution.py:158
  112.7 9.1 %gather_fusion.2 = f32[1024,8,8]{2,1,0:T(8,128)} fusion(f32[8,8,512]{1,0,2:T(8,128)S(1)} %bitcast.1085, s32[1024]{0:T(1024)S(1)} %get-tuple-element.367), kind=kCustom, calls=%fused_computation.2 | custom fusion | bytes 528384 | tf_op jit(solution)/shard_map/vmap()/gather | solution.py:157
  121.8 2.8 copy.567
  124.7 2.8 copy.561
  128.4 6.7 %psum.116 = f32[]{:T(128)} all-reduce(f32[]{:T(128)} %fusion.212), channel_id=1, replica_groups=mesh['chan_0'=4,'chan_1'=4,'stn_0'=4,'stn_1'=2] {'chan_0'}, use_global_device_ids=true, to_apply=%region_29.0 | all-reduce | flops 1 | bytes 8 | tf_op jit(solution)/shard_map/psum | solution.py:25
  135.1 6.7 %psum.117 = f32[]{:T(128)} all-reduce(f32[]{:T(128)} %psum.116), channel_id=1, replica_groups=mesh['chan_0'=4,'chan_1'=4,'stn_0'=4,'stn_1'=2] {'chan_1'}, use_global_device_ids=true, to_apply=%region_30.0 | all-reduce | flops 1 | bytes 8 | tf_op jit(solution)/shard_map/psum | solution.py:25
  141.8 7.6 %psum.118 = f32[]{:T(128)} all-reduce(f32[]{:T(128)} %psum.117), channel_id=1, replica_groups=mesh['chan_0'=4,'chan_1'=4,'stn_0'=4,'stn_1'=2] {'stn_0'}, use_global_device_ids=true, to_apply=%region_31.0 | all-reduce | flops 1 | bytes 8 | tf_op jit(solution)/shard_map/psum | solution.py:25
  149.4 9.1 %psum.119 = f32[]{:T(128)} all-reduce(f32[]{:T(128)} %psum.118), channel_id=1, replica_groups=mesh['chan_0'=4,'chan_1'=4,'stn_0'=4,'stn_1'=2] {'stn_1'}, use_global_device_ids=true, to_apply=%region_32.0 | all-reduce | flops 1 | bytes 8 | tf_op jit(solution)/shard_map/psum | solution.py:25
  163.0 2.5 scatter.15
  166.0 7.9 %all_to_all.36 = f32[8,1,6144]{2,1,0:T(1,128)S(1)} all-to-all(f32[8,1,6144]{2,1,0:T(1,128)S(1)} %reshape.20804), channel_id=1, replica_groups=mesh['chan_0'=4,'chan_1'=4,'stn_0'=4,'stn_1'=2] {'stn_0','stn_1'}, dimensions={0} | all-to-all | bytes 393216 | tf_op jit(solution)/shard_map/all_to_all | solution.py:36
  176.5 4.2 %all-to-all-start.3 = ((f32[8,1,4096]{2,1,0:T(1,128)}), f32[8,1,4096]{2,1,0:T(1,128)S(1)}, u32[]{:S(2)}, u32[]{:S(2)}) async-start(f32[8,1,4096]{2,1,0:T(1,128)} %reshape.20806), calls=%async_computation.3 | async-start | bytes 262144 | tf_op jit(solution)/shard_map/all_to_all | solution.py:42
  180.8 5.2 %all-to-all-done.3 = f32[8,1,4096]{2,1,0:T(1,128)S(1)} async-done(((f32[8,1,4096]{2,1,0:T(1,128)}), f32[8,1,4096]{2,1,0:T(1,128)S(1)}, u32[]{:S(2)}, u32[]{:S(2)}) %all-to-all-start.3) | async-done | bytes 131104 | tf_op jit(solution)/shard_map/all_to_all | solution.py:42
  187.8 9.1 %gather_fusion.5 = f32[1024,8,8]{2,1,0:T(8,128)} fusion(f32[8,8,512]{1,0,2:T(8,128)S(1)} %bitcast.1086, s32[1024]{0:T(1024)S(1)} %get-tuple-element.366), kind=kCustom, calls=%fused_computation.5 | custom fusion | bytes 528384 | tf_op jit(solution)/shard_map/vmap()/gather | solution.py:158
  196.9 9.1 %gather_fusion.4 = f32[1024,8,8]{2,1,0:T(8,128)} fusion(f32[8,8,512]{1,0,2:T(8,128)S(1)} %bitcast.1087, s32[1024]{0:T(1024)S(1)} %get-tuple-element.367), kind=kCustom, calls=%fused_computation.4 | custom fusion | bytes 528384 | tf_op jit(solution)/shard_map/vmap()/gather | solution.py:157
  206.0 2.8 copy.606
  208.9 2.8 copy.600
  212.6 19.9 %all-gather = f32[48,8,8,64]{3,2,1,0:T(8,128)S(1)} all-gather(f32[3,8,8,64]{3,2,1,0:T(8,128)S(1)} %broadcast_multiply_fusion.3), channel_id=2, replica_groups=mesh['chan_0'=4,'chan_1'=4,'stn_0'=4,'stn_1'=2] {'chan_0','chan_1'}, dimensions={0}, use_global_device_ids=true | all-gather | bytes 835584 | tf_op jit(solution)/shard_map/all_gather | solution.py:59
  232.5 8.4 %psum.120 = f32[]{:T(128)} all-reduce(f32[]{:T(128)} %fusion.211), channel_id=1, replica_groups=mesh['chan_0'=4,'chan_1'=4,'stn_0'=4,'stn_1'=2] {'chan_0'}, use_global_device_ids=true, to_apply=%region_43.0 | all-reduce | flops 1 | bytes 8 | tf_op jit(solution)/shard_map/psum | solution.py:25
  241.1 7.8 %psum.121 = f32[]{:T(128)} all-reduce(f32[]{:T(128)} %psum.120), channel_id=1, replica_groups=mesh['chan_0'=4,'chan_1'=4,'stn_0'=4,'stn_1'=2] {'chan_1'}, use_global_device_ids=true, to_apply=%region_44.0 | all-reduce | flops 1 | bytes 8 | tf_op jit(solution)/shard_map/psum | solution.py:25
  248.8 7.8 %psum.122 = f32[]{:T(128)} all-reduce(f32[]{:T(128)} %psum.121), channel_id=1, replica_groups=mesh['chan_0'=4,'chan_1'=4,'stn_0'=4,'stn_1'=2] {'stn_0'}, use_global_device_ids=true, to_apply=%region_45.0 | all-reduce | flops 1 | bytes 8 | tf_op jit(solution)/shard_map/psum | solution.py:25
  256.6 14.1 %psum.123 = f32[]{:T(128)} all-reduce(f32[]{:T(128)} %psum.122), channel_id=1, replica_groups=mesh['chan_0'=4,'chan_1'=4,'stn_0'=4,'stn_1'=2] {'stn_1'}, use_global_device_ids=true, to_apply=%region_46.0 | all-reduce | flops 1 | bytes 8 | tf_op jit(solution)/shard_map/psum | solution.py:25
  275.3 2.5 scatter.16
  278.9 3.3 all-to-all-start.4
  282.7 4.4 %all-to-all-done.4 = f32[8,1,6144]{2,1,0:T(1,128)S(1)} async-done(((f32[8,1,6144]{2,1,0:T(1,128)}), f32[8,1,6144]{2,1,0:T(1,128)S(1)}, u32[]{:S(2)}, u32[]{:S(2)}) %all-to-all-start.4) | async-done | bytes 196640 | tf_op jit(solution)/shard_map/all_to_all | solution.py:36
  289.0 8.7 %all_to_all.37 = f32[8,1,4096]{2,1,0:T(1,128)S(1)} all-to-all(f32[8,1,4096]{2,1,0:T(1,128)S(1)} %reshape.20810), channel_id=1, replica_groups=mesh['chan_0'=4,'chan_1'=4,'stn_0'=4,'stn_1'=2] {'stn_0','stn_1'}, dimensions={0} | all-to-all | bytes 262144 | tf_op jit(solution)/shard_map/all_to_all | solution.py:42
  299.5 9.1 %gather_fusion.7 = f32[1024,8,8]{2,1,0:T(8,128)} fusion(f32[8,8,512]{1,0,2:T(8,128)S(1)} %bitcast.1082, s32[1024]{0:T(1024)S(1)} %get-tuple-element.366), kind=kCustom, calls=%fused_computation.7 | custom fusion | bytes 528384 | tf_op jit(solution)/shard_map/vmap()/gather | solution.py:158
  308.6 9.1 %gather_fusion.6 = f32[1024,8,8]{2,1,0:T(8,128)} fusion(f32[8,8,512]{1,0,2:T(8,128)S(1)} %bitcast.1083, s32[1024]{0:T(1024)S(1)} %get-tuple-element.367), kind=kCustom, calls=%fused_computation.6 | custom fusion | bytes 528384 | tf_op jit(solution)/shard_map/vmap()/gather | solution.py:157
  317.7 2.8 copy.621
  320.6 2.8 copy.615
  324.3 6.9 %psum.124 = f32[]{:T(128)} all-reduce(f32[]{:T(128)} %fusion.210), channel_id=1, replica_groups=mesh['chan_0'=4,'chan_1'=4,'stn_0'=4,'stn_1'=2] {'chan_0'}, use_global_device_ids=true, to_apply=%region_58.0 | all-reduce | flops 1 | bytes 8 | tf_op jit(solution)/shard_map/psum | solution.py:25
  331.2 6.6 %psum.125 = f32[]{:T(128)} all-reduce(f32[]{:T(128)} %psum.124), channel_id=1, replica_groups=mesh['chan_0'=4,'chan_1'=4,'stn_0'=4,'stn_1'=2] {'chan_1'}, use_global_device_ids=true, to_apply=%region_59.0 | all-reduce | flops 1 | bytes 8 | tf_op jit(solution)/shard_map/psum | solution.py:25
  337.8 7.5 %psum.126 = f32[]{:T(128)} all-reduce(f32[]{:T(128)} %psum.125), channel_id=1, replica_groups=mesh['chan_0'=4,'chan_1'=4,'stn_0'=4,'stn_1'=2] {'stn_0'}, use_global_device_ids=true, to_apply=%region_60.0 | all-reduce | flops 1 | bytes 8 | tf_op jit(solution)/shard_map/psum | solution.py:25
  345.3 9.6 %psum.127 = f32[]{:T(128)} all-reduce(f32[]{:T(128)} %psum.126), channel_id=1, replica_groups=mesh['chan_0'=4,'chan_1'=4,'stn_0'=4,'stn_1'=2] {'stn_1'}, use_global_device_ids=true, to_apply=%region_61.0 | all-reduce | flops 1 | bytes 8 | tf_op jit(solution)/shard_map/psum | solution.py:25
  357.3 2.2 fusion.10
  359.6 2.6 scatter.19
  362.6 7.9 %all_to_all.38 = f32[8,1,6144]{2,1,0:T(1,128)S(1)} all-to-all(f32[8,1,6144]{2,1,0:T(1,128)S(1)} %reshape.20812), channel_id=1, replica_groups=mesh['chan_0'=4,'chan_1'=4,'stn_0'=4,'stn_1'=2] {'stn_0','stn_1'}, dimensions={0} | all-to-all | bytes 393216 | tf_op jit(solution)/shard_map/all_to_all | solution.py:36
  372.8 20.1 %all-gather.1 = f32[48,8,8,64]{3,2,1,0:T(8,128)S(1)} all-gather(f32[3,8,8,64]{3,2,1,0:T(8,128)S(1)} %broadcast_multiply_fusion), channel_id=3, replica_groups=mesh['chan_0'=4,'chan_1'=4,'stn_0'=4,'stn_1'=2] {'chan_0','chan_1'}, dimensions={0}, use_global_device_ids=true | all-gather | bytes 835584 | tf_op jit(solution)/shard_map/all_gather | solution.py:59
  (260 shorter events, 47.2 us)
Async XLA Ops:
  0.6 28.0 %copy-start = (f32[1,8,16,1024]{3,2,1,0:T(8,128)S(1)}, f32[1,8,16,1024]{3,2,1,0:T(8,128)}, u32[]{:S(2)}) copy-start(f32[1,8,16,1024]{3,2,1,0:T(8,128)} %param.17) | copy-start | bytes 1572868
  14.0 14.7 %copy-start.10 = (s32[16,1]{0,1:T(1,128)S(1)}, s32[16,1]{0,1:T(1,128)}, u32[]{:S(2)}) copy-start(s32[16,1]{0,1:T(1,128)} %param.18) | copy-start | bytes 196
  25.9 3.5 copy-start.2
  25.9 14.3 %copy-start.11 = (s32[3]{0:T(128)S(1)}, s32[3]{0:T(128)}, u32[]{:S(2)}) copy-start(s32[3]{0:T(128)} %constant.148.clone.1) | copy-start | bytes 40
  29.2 42.0 %copy-start.9 = (s32[4]{0:T(128)S(1)}, s32[4]{0:T(128)}, u32[]{:S(2)}) copy-start(s32[4]{0:T(128)} %constant.149.clone.1) | copy-start | bytes 52
  70.6 18.7 %copy-start.3 = (f32[3,8,8,512]{3,2,1,0:T(8,128)S(1)}, f32[3,8,8,512]{3,2,1,0:T(8,128)}, u32[]{:S(2)}) copy-start(f32[3,8,8,512]{3,2,1,0:T(8,128)} %param.21) | copy-start | bytes 1179652
  70.9 21.5 %copy-start.6 = (f32[1,8,8,512]{3,2,1,0:T(8,128)S(1)}, f32[1,8,8,512]{3,2,1,0:T(8,128)}, u32[]{:S(2)}) copy-start(f32[1,8,8,512]{3,2,1,0:T(8,128)} %param.22) | copy-start | bytes 393220
  70.9 21.5 %copy-start.8 = (f32[8]{0:T(128)S(1)}, f32[8]{0:T(128)}, u32[]{:S(2)}) copy-start(f32[8]{0:T(128)} %param.23) | copy-start | bytes 100
  70.9 21.8 %copy-start.5 = (f32[1,8,8,512]{3,2,1,0:T(8,128)S(1)}, f32[1,8,8,512]{3,2,1,0:T(8,128)}, u32[]{:S(2)}) copy-start(f32[1,8,8,512]{3,2,1,0:T(8,128)} %param.20) | copy-start | bytes 393220
  79.3 11.2 %all-to-all-start = ((f32[8,1,6144]{2,1,0:T(1,128)}), f32[8,1,6144]{2,1,0:T(1,128)S(1)}, u32[]{:S(2)}, u32[]{:S(2)}) async-start(f32[8,1,6144]{2,1,0:T(1,128)} %reshape.20800), calls=%async_computation | async-start | bytes 393216 | tf_op jit(solution)/shard_map/all_to_all | solution.py:36
  176.5 9.5 %all-to-all-start.3 = ((f32[8,1,4096]{2,1,0:T(1,128)}), f32[8,1,4096]{2,1,0:T(1,128)S(1)}, u32[]{:S(2)}, u32[]{:S(2)}) async-start(f32[8,1,4096]{2,1,0:T(1,128)} %reshape.20806), calls=%async_computation.3 | async-start | bytes 262144 | tf_op jit(solution)/shard_map/all_to_all | solution.py:42
  271.9 16.6 %copy-start.7 = (f32[1,8,8,512]{3,2,1,0:T(8,128)S(1)}, f32[1,8,8,512]{3,2,1,0:T(8,128)}, u32[]{:S(2)}) copy-start(f32[1,8,8,512]{3,2,1,0:T(8,128)} %param.22) | copy-start | bytes 393220
  278.9 8.1 %all-to-all-start.4 = ((f32[8,1,6144]{2,1,0:T(1,128)}), f32[8,1,6144]{2,1,0:T(1,128)S(1)}, u32[]{:S(2)}, u32[]{:S(2)}) async-start(f32[8,1,6144]{2,1,0:T(1,128)} %reshape.20808), calls=%async_computation.4 | async-start | bytes 393216 | tf_op jit(solution)/shard_map/all_to_all | solution.py:36
  359.5 34.5 %copy-start.1 = (f32[1,8,16,1024]{3,2,1,0:T(8,128)S(1)}, f32[1,8,16,1024]{3,2,1,0:T(8,128)}, u32[]{:S(2)}) copy-start(f32[1,8,16,1024]{3,2,1,0:T(8,128)} %param.17) | copy-start | bytes 1572868
  393.0 1.0 copy-start.4
where the time goes:
time: 399 us; the launch traced here: 394 us
  blocking collectives  211 us (53%)
  local copies, waits for them, and re-layouts  117 us (29%)
  other arithmetic  22.6 us (6%)
  matrix products  14.8 us (4%)
  starting transfers between devices  10.9 us (3%)
  waiting for transfers between devices  9.64 us (2%)
  between operations  8.02 us (2%)
    psum x16, blocking collectives, over_axes(): value = lax.psum(value, axis)  138 us
    gather x8, local copies, waits for them, and re-layouts, channel_state(): second_gain = entries(spectral_jones_matrices[:, :, antenna_pairs[1]])  47.6 us
    gather x8, local copies, waits for them, and re-layouts, channel_state(): first_gain = entries(spectral_jones_matrices[:, :, antenna_pairs[0]])  47.5 us
    all_gather x2, blocking collectives, over_pieces(): return lax.all_gather(value, axis).sum(0)  40 us
    all_to_all x2, blocking collectives, copy_for_each(): lax.all_to_all(jnp.broadcast_to(value[None], (length, *value.shape)), axi...  17.5 us
    all_to_all x2, blocking collectives, sent_and_summed(): lax.all_to_all(split_up(value, dim, length), axis, 0, 0, tiled=True)  15.9 us
    scatter x4, local copies, waits for them, and re-layouts, channel_sums(): lax.dynamic_update_slice_in_dim(every_station, own_rows, block_start, 2)  10 us
    dot_general x4, matrix products, channel_sums(): jnp.einsum('pkb,bs->pks', first_parts, first_table, precision=highest)  8.77 us
  transfers between devices with their start and end apart: 3, of which 2 were waited for; matrix products, arithmetic and copies ran while one was open for 1% of the time, Pallas kernels for 0%

commit v1 on v0

v1 whole, which is shorter than its diff:
```python
import numpy as np
import jax
import jax.numpy as jnp
from jax import lax
from jax.experimental import pallas as pl
from jax.experimental.pallas import tpu as pltpu
from jax.sharding import PartitionSpec as P

PATHS = 8
SOURCES = 16
TERMS = 3
STEPS = 2
INNER = 2
PASSES = STEPS * INNER
NU = 2.0
TINY = 1e-06
MESH = pl.DeviceIdType.MESH
WIDE = 128
PAIRS = ((0, 1), (2, 3), (4, 8), (5, 9), (6, 10), (7, 11))
bf16 = jnp.bfloat16
f32 = jnp.float32


def basis_table(count):
    frequency = (2.0 * np.arange(count, dtype=np.float32) + 1.0) / np.float32(count) - 1.0
    columns = []
    for degree in range(TERMS):
        column = (frequency**degree).astype(np.float32)
        for earlier in columns:
            column = column - np.sum(earlier * column) / np.float32(count) * earlier
        column = column / np.sqrt(np.sum(column * column) / np.float32(count))
        columns.append(column.astype(np.float32))
    return np.stack(columns, axis=1)


def mul(a, b):
    return (a[0] * b[0] - a[1] * b[1], a[0] * b[1] + a[1] * b[0])


def mul_conj(a, b):
    return (a[0] * b[0] + a[1] * b[1], a[1] * b[0] - a[0] * b[1])


def conj_mul(a, b):
    return (a[0] * b[0] + a[1] * b[1], a[0] * b[1] - a[1] * b[0])


def add(a, b):
    return (a[0] + b[0], a[1] + b[1])


def product(a, b):
    return [
        add(mul(a[0], b[0]), mul(a[1], b[2])),
        add(mul(a[0], b[1]), mul(a[1], b[3])),
        add(mul(a[2], b[0]), mul(a[3], b[2])),
        add(mul(a[2], b[1]), mul(a[3], b[3])),
    ]


def product_with_adjoint(a, b):
    return [
        add(mul_conj(a[0], b[0]), mul_conj(a[1], b[1])),
        add(mul_conj(a[0], b[2]), mul_conj(a[1], b[3])),
        add(mul_conj(a[2], b[0]), mul_conj(a[3], b[1])),
        add(mul_conj(a[2], b[2]), mul_conj(a[3], b[3])),
    ]


def adjoint_product(a, b):
    return [
        add(conj_mul(a[0], b[0]), conj_mul(a[2], b[2])),
        add(conj_mul(a[0], b[1]), conj_mul(a[2], b[3])),
        add(conj_mul(a[1], b[0]), conj_mul(a[3], b[2])),
        add(conj_mul(a[1], b[1]), conj_mul(a[3], b[3])),
    ]


def power(a):
    return a[0] * a[0] + a[1] * a[1]


def gram(y):
    cross = add(mul_conj(y[0], y[2]), mul_conj(y[1], y[3]))
    return [power(y[0]) + power(y[1]), power(y[2]) + power(y[3]), cross[0], cross[1]]


def gram_of_adjoint(h):
    cross = add(conj_mul(h[0], h[1]), conj_mul(h[2], h[3]))
    return [power(h[0]) + power(h[2]), power(h[1]) + power(h[3]), cross[0], cross[1]]


def halves(x):
    top = x.astype(bf16)
    return top, (x - top.astype(f32)).astype(bf16)


def swap(x):
    return pltpu.roll(x, 64, 1)


def low(shape):
    return lax.broadcasted_iota(jnp.int32, shape, 1) < 64


def kernel(
    chans,
    blocks,
    table,
    pointing,
    rhos,
    vis_hbm,
    model_hbm,
    pairs_hbm,
    gain_hbm,
    poly_hbm,
    dual_hbm,
    gain_out,
    dual_out,
    fit_out,
    vis,
    model,
    pairs,
    gain_tile,
    poly_tile,
    dual_tile,
    whole,
    coherent,
    spread_q,
    collect_q,
    spread_p,
    collect_p,
    gain_p,
    gain_q,
    back,
    toward,
    target,
    energy,
    parts_p,
    parts_q,
    wide_p,
    wide_q,
    gain,
    dual,
    anchor,
    e_src,
    e_row,
    e_stn,
    e_chan,
    sums_src,
    sums,
    gains_src,
    gains,
    fits_src,
    fits,
    load_sem,
    e_sem,
    s_sem,
    g_sem,
    f_sem,
):
    chan = lax.axis_index("chan")
    stn = lax.axis_index("stn")
    baselines = vis.shape[1]
    stations = whole.shape[1]
    chunks = baselines // WIDE
    samples = float(chans * blocks * baselines)

    def stn_peer(d):
        return lax.rem(stn + d, blocks)

    def chan_peer(d):
        return lax.rem(chan + d, chans)

    barrier = pltpu.get_barrier_semaphore()

    def greet_stn(d, _):
        pl.semaphore_signal(barrier, inc=1, device_id=(chan, stn_peer(d)), device_id_type=MESH)
        return 0

    def greet_chan(d, _):
        pl.semaphore_signal(barrier, inc=1, device_id=(chan_peer(d), stn), device_id_type=MESH)
        return 0

    lax.fori_loop(1, blocks, greet_stn, 0)
    lax.fori_loop(1, chans, greet_chan, 0)

    lane_start = pl.multiple_of(lax.div(stn, 2) * 128, 128)
    loads = [
        pltpu.make_async_copy(pairs_hbm, pairs, load_sem.at[0]),
        pltpu.make_async_copy(model_hbm, model, load_sem.at[1]),
        pltpu.make_async_copy(gain_hbm.at[:, pl.ds(lane_start, 128)], gain_tile, load_sem.at[2]),
        pltpu.make_async_copy(gain_hbm, whole, load_sem.at[3]),
        pltpu.make_async_copy(vis_hbm, vis, load_sem.at[4]),
        pltpu.make_async_copy(poly_hbm.at[:, pl.ds(lane_start, 128)], poly_tile, load_sem.at[5]),
        pltpu.make_async_copy(dual_hbm.at[:, pl.ds(lane_start, 128)], dual_tile, load_sem.at[6]),
    ]
    for copy in loads:
        copy.start()

    loads[0].wait()
    first = pairs[0:1, :] - stn * 64
    second = pairs[1:2, :]
    row = lax.broadcasted_iota(jnp.int32, (128, baselines), 0)
    spread_p[...] = jnp.where(row == first, 1.0, 0.0).astype(bf16)
    for j in range(stations // 128):
        spread_q[128 * j : 128 * j + 128, :] = jnp.where(row + 128 * j == second, 1.0, 0.0).astype(bf16)
    column = lax.broadcasted_iota(jnp.int32, (baselines, 128), 1).astype(f32)
    first_t = jnp.broadcast_to(first.astype(f32), (128, baselines)).T
    second_t = jnp.broadcast_to(second.astype(f32), (128, baselines)).T
    collect_p[...] = jnp.where(column == first_t, 1.0, 0.0).astype(bf16)
    for j in range(stations // 128):
        collect_q[:, 128 * j : 128 * j + 128] = jnp.where(
            column + 128.0 * j == second_t, 1.0, 0.0
        ).astype(bf16)

    lane = lax.broadcasted_iota(jnp.int32, (64, 128), 1)
    high_row = lax.broadcasted_iota(jnp.int32, (64, 128), 0)
    point = jnp.zeros((64, 128), jnp.int32)
    for s in range(SOURCES):
        point = jnp.where(lane % SOURCES == s, pointing[s], point)
    member = jnp.where(
        (high_row // PATHS == lane // SOURCES) & (high_row % PATHS == point), 1.0, 0.0
    ).astype(bf16)
    loads[1].wait()

    def combine(i, _):
        at = pl.ds(pl.multiple_of(i * 256, 256), 256)
        m = model[:, at]
        m0 = m.astype(bf16)
        rest = m - m0.astype(f32)
        m1 = rest.astype(bf16)
        m2 = (rest - m1.astype(f32)).astype(bf16)
        coherent[:, at] = (
            jnp.dot(member, m0, preferred_element_type=f32)
            + jnp.dot(member, m1, preferred_element_type=f32)
            + jnp.dot(member, m2, preferred_element_type=f32)
        )
        return 0

    lax.fori_loop(0, baselines // 256, combine, 0)

    low_32 = low((32, 128))

    def own(re, im):
        return jnp.where(
            lax.rem(stn, 2) == 0,
            jnp.where(low_32, re, swap(im)),
            jnp.where(low_32, swap(re), im),
        )

    def mine(t):
        value = f32(0.0)
        for f in range(chans):
            value = jnp.where(chan == f, f32(table[f, t]), value)
        return value

    my_basis = [mine(t) for t in range(TERMS)]
    for copy in loads[2:]:
        copy.wait()
    gain[...] = own(gain_tile[0:32, :], gain_tile[32:64, :])
    dual[...] = own(dual_tile[0:32, :], dual_tile[32:64, :])
    start = jnp.zeros((32, 128), f32)
    for t in range(TERMS):
        start = start + my_basis[t] * own(
            poly_tile[64 * t : 64 * t + 32, :], poly_tile[64 * t + 32 : 64 * t + 64, :]
        )
    anchor[...] = start - dual[...]

    k_row = lax.broadcasted_iota(jnp.int32, (PATHS, 128), 0)
    rho = jnp.zeros((PATHS, 128), f32)
    for k in range(PATHS):
        rho = jnp.where(k_row == k, rhos[k], rho)
    low_8 = low((8, 128))

    pl.semaphore_wait(barrier, blocks + chans - 2)

    def entries(ref, at):
        return [(ref[8 * i : 8 * i + 8, at], ref[32 + 8 * i : 40 + 8 * i, at]) for i in range(4)]

    def keep(ref, at, values):
        for i in range(4):
            ref[8 * i : 8 * i + 8, at] = values[i][0]
            ref[32 + 8 * i : 40 + 8 * i, at] = values[i][1]

    def chunk(i):
        return pl.ds(pl.multiple_of(i * WIDE, WIDE), WIDE)

    def wait_all(ref, sem):
        pltpu.make_async_copy(ref, ref, sem).wait()

    def to_stn(src, dst, sem):
        def send(d, _):
            pltpu.make_async_remote_copy(
                src_ref=src(stn_peer(d)),
                dst_ref=dst,
                send_sem=sem.at[0],
                recv_sem=sem.at[1],
                device_id=(chan, stn_peer(d)),
                device_id_type=MESH,
            ).start()
            return 0

        lax.fori_loop(1, blocks, send, 0)

    def to_chan(src, dst, sem):
        def send(d, _):
            pltpu.make_async_remote_copy(
                src_ref=src,
                dst_ref=dst,
                send_sem=sem.at[0],
                recv_sem=sem.at[1],
                device_id=(chan_peer(d), stn),
                device_id_type=MESH,
            ).start()
            return 0

        lax.fori_loop(1, chans, send, 0)

    def fit_of(step):
        wait_all(fits.at[step, pl.ds(0, chans - 1)], f_sem.at[step, 1])
        got = [jnp.zeros((32, 128), f32)] * TERMS
        for f in range(chans):
            value = fits[step, f]
            got = [got[t] + f32(table[f, t]) * value for t in range(TERMS)]
        return [g * f32(1.0 / chans) for g in got]

    def consensus_of(fit):
        value = my_basis[0] * fit[0]
        for t in range(1, TERMS):
            value = value + my_basis[t] * fit[t]
        return value

    def one_pass(it, _):
        packed = gain[...]
        top, rest = halves(jnp.concatenate([packed, swap(packed)], axis=0))
        both = jnp.dot(
            jnp.concatenate([top, rest], axis=0), spread_p[...], preferred_element_type=f32
        )
        gain_p[...] = both[0:64] + both[64:128]

        def back_terms(i, _):
            at = chunk(i)
            h = product(entries(gain_p, at), entries(coherent, at))
            keep(back, at, h)
            for n, part in enumerate(gram_of_adjoint(h)):
                parts_q[8 * n : 8 * n + 8, at] = part
            return 0

        lax.fori_loop(0, chunks, back_terms, 0)

        @pl.when(it > 0)
        def _():
            wait_all(gains.at[it - 1, pl.ds(0, blocks - 1)], g_sem.at[it - 1, 1])
            for j in range(blocks // 2):
                a = gains[it - 1, 2 * j]
                b = gains[it - 1, 2 * j + 1]
                whole[0:32, 128 * j : 128 * j + 128] = jnp.where(low_32, a, swap(b))
                whole[32:64, 128 * j : 128 * j + 128] = jnp.where(low_32, swap(a), b)

        top, rest = halves(whole[...])
        both = jnp.dot(
            jnp.concatenate([top, rest], axis=0), spread_q[...], preferred_element_type=f32
        )
        gain_q[...] = both[0:64] + both[64:128]

        def residuals(i, total):
            at = chunk(i)
            y = product_with_adjoint(entries(coherent, at), entries(gain_q, at))
            keep(toward, at, y)
            g = product(entries(gain_p, at), y)
            x = []
            e = None
            for n in range(4):
                pair = []
                for part in range(2):
                    value = g[n][part]
                    left = vis[n + 4 * part : n + 4 * part + 1, at] - jnp.sum(value, axis=0, keepdims=True)
                    e = left * left if e is None else e + left * left
                    pair.append(left + value)
                x.append(tuple(pair))
            keep(target, at, x)
            energy[:, at] = e
            return total + e

        total = lax.fori_loop(0, chunks, residuals, jnp.zeros((1, WIDE), f32))
        e_src[it] = total
        e_stn[it, stn] = total
        to_stn(lambda _: e_src.at[it], e_stn.at[it, stn], e_sem.at[0, it])

        def sums_of(i):
            at = chunk(i)
            y, x, h = entries(toward, at), entries(target, at), entries(back, at)
            b = product_with_adjoint(x, y)
            for n, part in enumerate(gram(y) + [v[0] for v in b] + [v[1] for v in b]):
                parts_p[8 * n : 8 * n + 8, at] = part
            b = adjoint_product(x, h)
            for n, part in enumerate([v[0] for v in b] + [v[1] for v in b]):
                parts_q[32 + 8 * n : 40 + 8 * n, at] = part

        def early(i, _):
            sums_of(i)
            return 0

        lax.fori_loop(0, chunks // 2, early, 0)
        wait_all(e_stn.at[it, pl.ds(0, blocks - 1)], e_sem.at[0, it, 1])
        total = e_stn[it, 0]
        for n in range(1, blocks):
            total = total + e_stn[it, n]
        e_row[it] = total
        e_chan[it, chan] = total
        to_chan(e_row.at[it], e_chan.at[it, chan], e_sem.at[1, it])
        lax.fori_loop(chunks // 2, chunks, early, 0)
        wait_all(e_chan.at[it, pl.ds(0, chans - 1)], e_sem.at[1, it, 1])
        total = e_chan[it, 0]
        for n in range(1, chans):
            total = total + e_chan[it, n]
        noise = jnp.sum(total, axis=1, keepdims=True) * f32(1.0 / samples) + TINY
        scale = jnp.broadcast_to(1.0 / noise, (1, WIDE))

        def weigh(i, _):
            at = chunk(i)
            weight = (NU + 2.0) / (NU + energy[:, at] * scale)
            for n in range(6):
                top, rest = halves(parts_q[16 * n : 16 * n + 16, at] * weight)
                wide_q[16 * n : 16 * n + 16, at] = top
                wide_q[96 + 16 * n : 112 + 16 * n, at] = rest
                top, rest = halves(parts_p[16 * n : 16 * n + 16, at] * weight)
                wide_p[16 * n : 16 * n + 16, at] = top
                wide_p[96 + 16 * n : 112 + 16 * n, at] = rest
            return 0

        lax.fori_loop(0, chunks, weigh, 0)
        for j in range(blocks // 2):
            both = jnp.dot(
                wide_q[...], collect_q[:, 128 * j : 128 * j + 128], preferred_element_type=f32
            )
            both = both[0:96] + both[96:192]
            for n, (a, b) in enumerate(PAIRS):
                a, b = both[8 * a : 8 * a + 8], both[8 * b : 8 * b + 8]
                sums_src[it, 2 * j, 8 * n : 8 * n + 8, :] = jnp.where(low_8, a, swap(b))
                sums_src[it, 2 * j + 1, 8 * n : 8 * n + 8, :] = jnp.where(low_8, swap(a), b)
        to_stn(lambda peer: sums_src.at[it, peer], sums.at[it, stn], s_sem.at[it])
        both = jnp.dot(wide_p[...], collect_p[...], preferred_element_type=f32)
        both = both[0:96] + both[96:192]
        for n, (a, b) in enumerate(PAIRS):
            a, b = both[8 * a : 8 * a + 8], both[8 * b : 8 * b + 8]
            sums[it, stn, 8 * n : 8 * n + 8, :] = (
                jnp.where(low_8, a, swap(b)) + sums_src[it, stn, 8 * n : 8 * n + 8, :]
            )

        @pl.when(it == INNER)
        def _():
            consensus = consensus_of(fit_of(0))
            after = dual[...] + gain[...] - consensus
            dual[...] = after
            anchor[...] = consensus - after

        wait_all(sums.at[it, pl.ds(0, blocks - 1)], s_sem.at[it, 1])
        got = sums[it, 0]
        for n in range(1, blocks):
            got = got + sums[it, n]
        diag, cross = got[0:8], got[8:16]
        d1, d2 = diag + rho, swap(diag) + rho
        cr, ci = cross, swap(cross)
        over = 1.0 / (d1 * d2 - cr * cr - ci * ci)
        right = []
        for n in range(4):
            value = got[16 + 8 * n : 24 + 8 * n] + rho * anchor[8 * n : 8 * n + 8, :]
            right.append((value, swap(value)))
        up = (cr * over, ci * over)
        s1, s2 = d2 * over, d1 * over
        solved = []
        for r in range(2):
            x, y = right[2 * r], right[2 * r + 1]
            one = mul_conj(y, up)
            two = mul(x, up)
            solved.append((x[0] * s1 - one[0], x[1] * s1 - one[1]))
            solved.append((y[0] * s2 - two[0], y[1] * s2 - two[1]))
        for n in range(4):
            value = 0.5 * (gain[8 * n : 8 * n + 8, :] + jnp.where(low_8, solved[n][0], swap(solved[n][1])))
            gain[8 * n : 8 * n + 8, :] = value

        @pl.when(it < PASSES - 1)
        def _():
            gains_src[it] = gain[...]
            gains[it, stn] = gain[...]
            to_stn(lambda _: gains_src.at[it], gains.at[it, stn], g_sem.at[it])

        @pl.when(lax.rem(it, INNER) == INNER - 1)
        def _():
            step = lax.div(it, INNER)
            fits_src[step] = gain[...] + dual[...]
            fits[step, chan] = gain[...] + dual[...]
            to_chan(fits_src.at[step], fits.at[step, chan], f_sem.at[step])

        return 0

    lax.fori_loop(0, PASSES, one_pass, 0)

    fit = fit_of(STEPS - 1)
    consensus = consensus_of(fit)
    final = gain[...]
    after = dual[...] + final - consensus
    gain_out[0:32, :] = final[:, 0:64]
    gain_out[32:64, :] = swap(final)[:, 0:64]
    dual_out[0:32, :] = after[:, 0:64]
    dual_out[32:64, :] = swap(after)[:, 0:64]
    for t in range(TERMS):
        fit_out[64 * t : 64 * t + 32, :] = fit[t][:, 0:64]
        fit_out[64 * t + 32 : 64 * t + 64, :] = swap(fit[t])[:, 0:64]

    def sent(it, _):
        wait_all(e_stn.at[it, pl.ds(0, blocks - 1)], e_sem.at[0, it, 0])
        wait_all(e_chan.at[it, pl.ds(0, chans - 1)], e_sem.at[1, it, 0])
        wait_all(sums.at[it, pl.ds(0, blocks - 1)], s_sem.at[it, 0])
        return 0

    def sent_gains(it, _):
        wait_all(gains.at[it, pl.ds(0, blocks - 1)], g_sem.at[it, 0])
        return 0

    def sent_fits(step, _):
        wait_all(fits.at[step, pl.ds(0, chans - 1)], f_sem.at[step, 0])
        return 0

    lax.fori_loop(0, PASSES, sent, 0)
    lax.fori_loop(0, PASSES - 1, sent_gains, 0)
    lax.fori_loop(0, STEPS, sent_fits, 0)


def solution(mesh):
    chans, blocks = mesh.shape["chan"], mesh.shape["stn"]
    table = basis_table(chans)

    def body(vis, model, pointing, pairs, gains, poly, dual, rhos):
        baselines = vis.shape[2]
        stations = gains.shape[3]

        def run(*refs):
            kernel(chans, blocks, table, *refs)

        any_spec = pl.BlockSpec(memory_space=pl.ANY)
        smem = pl.BlockSpec(memory_space=pltpu.SMEM)
        vmem = pl.BlockSpec(memory_space=pltpu.VMEM)
        dma = pltpu.SemaphoreType.DMA
        big = lambda rows, dtype=f32: pltpu.VMEM((rows, baselines), dtype)
        state = pltpu.VMEM((32, 128), f32)
        out = pl.pallas_call(
            run,
            out_shape=(
                jax.ShapeDtypeStruct((64, 64), f32),
                jax.ShapeDtypeStruct((64, 64), f32),
                jax.ShapeDtypeStruct((64 * TERMS, 64), f32),
            ),
            in_specs=[smem, smem] + [any_spec] * 6,
            out_specs=(vmem, vmem, vmem),
            scratch_shapes=[
                big(8),
                big(128),
                pltpu.VMEM((2, baselines), jnp.int32),
                pltpu.VMEM((64, 128), f32),
                pltpu.VMEM((64 * TERMS, 128), f32),
                pltpu.VMEM((64, 128), f32),
                pltpu.VMEM((64, stations), f32),
                big(64),
                big(stations, bf16),
                pltpu.VMEM((baselines, stations), bf16),
                big(128, bf16),
                pltpu.VMEM((baselines, 128), bf16),
                big(64),
                big(64),
                big(64),
                big(64),
                big(64),
                big(1),
                big(96),
                big(96),
                big(192, bf16),
                big(192, bf16),
                state,
                state,
                state,
                pltpu.VMEM((PASSES, 1, 128), f32),
                pltpu.VMEM((PASSES, 1, 128), f32),
                pltpu.VMEM((PASSES, blocks, 1, 128), f32),
                pltpu.VMEM((PASSES, chans, 1, 128), f32),
                pltpu.VMEM((PASSES, blocks, 48, 128), f32),
                pltpu.VMEM((PASSES, blocks, 48, 128), f32),
                pltpu.VMEM((PASSES - 1, 32, 128), f32),
                pltpu.VMEM((PASSES - 1, blocks, 32, 128), f32),
                pltpu.VMEM((STEPS, 32, 128), f32),
                pltpu.VMEM((STEPS, chans, 32, 128), f32),
                dma((7,)),
                dma((2, PASSES, 2)),
                dma((PASSES, 2)),
                dma((PASSES - 1, 2)),
                dma((STEPS, 2)),
            ],
            compiler_params=pltpu.CompilerParams(
                collective_id=0, has_side_effects=True, vmem_limit_bytes=40 << 20
            ),
            name="calibrate",
        )(
            pointing.reshape(SOURCES),
            rhos,
            vis.reshape(8, baselines),
            model.reshape(8 * SOURCES, baselines),
            pairs,
            gains.reshape(64, stations),
            poly.reshape(64 * TERMS, stations),
            dual.reshape(64, stations),
        )
        return (
            out[0].reshape(1, 8, PATHS, 64),
            out[1].reshape(1, 8, PATHS, 64),
            out[2].reshape(TERMS, 8, PATHS, 64),
        )

    return jax.shard_map(
        body,
        mesh=mesh,
        in_specs=(
            P("chan", None, "stn"),
            P("chan", None, None, "stn"),
            P(),
            P(None, "stn"),
            P("chan", None, None, None),
            P(),
            P("chan", None, None, None),
            P(),
        ),
        out_specs=(
            P("chan", None, None, "stn"),
            P("chan", None, None, "stn"),
            P(None, None, None, "stn"),
        ),
        check_vma=False,
    )
```

time: 399 us -> 90.7 us (0.23); the launches traced: 394 us -> 90.3 us
  blocking collectives: 211 us -> 0 us
  local copies, waits for them, and re-layouts: 117 us -> 7.15 us
  Pallas kernels: 0 us -> 82.5 us
  other arithmetic: 22.6 us -> 0 us
  matrix products: 14.8 us -> 0 us
  starting transfers between devices: 10.9 us -> 0 us
  waiting for transfers between devices: 9.64 us -> 0 us
  between operations: 8.02 us -> 0.67 us
    psum x16 -> x0, blocking collectives: 138 us -> none  [over_axes(): value = lax.psum(value, axis)]
    gather x16 -> x0, local copies, waits for them, and re-layouts: 95.1 us -> none  [the longest x8 47.6 us: channel_state(): second_gain = entries(spectral_jones_matrices[:, :, antenna_pairs[1]])]
    pallas_call x0 -> x1, Pallas kernels: none -> 82.5 us  [body(): pl.pallas_call(run, out_shape=(jax.ShapeDtypeStruct((64, 64), f32), jax.S...]
    all_gather x2 -> x0, blocking collectives: 40 us -> none  [over_pieces(): return lax.all_gather(value, axis).sum(0)]
    all_to_all x4 -> x0, blocking collectives: 33.4 us -> none  [the longest x2 17.5 us: copy_for_each(): lax.all_to_all(jnp.broadcast_to(value[None], (length, *value.shape)), axi...]
    dot_general x12 -> x0, matrix products: 14.8 us -> none  [the longest x4 8.77 us: channel_sums(): jnp.einsum('pkb,bs->pks', first_parts, first_table, precision=highest)]
    all_to_all x3 -> x0, starting transfers between devices: 10.9 us -> none  [the longest x2 6.68 us: sent_and_summed(): lax.all_to_all(split_up(value, dim, length), axis, 0, 0, tiled=True)]
    scatter x4 -> x0, local copies, waits for them, and re-layouts: 10 us -> none  [channel_sums(): lax.dynamic_update_slice_in_dim(every_station, own_rows, block_start, 2)]
  transfers between devices with their start and end apart: 3 -> 0, of which waited for: 2 -> 0; matrix products, arithmetic and copies ran while one was open for 1% -> 0% of each run, Pallas kernels for 0% -> 0%
where the time goes in v1:
time: 90.7 us; the launch traced here: 90.3 us
  Pallas kernels  82.5 us (91%)
  local copies, waits for them, and re-layouts  7.15 us (8%)
    pallas_call x1, Pallas kernels, body(): pl.pallas_call(run, out_shape=(jax.ShapeDtypeStruct((64, 64), f32), jax.S...  82.5 us
    unnamed x19, local copies, waits for them, and re-layouts  7.15 us

profile of v1, /device:TPU:1, one launch (start us, length us, event | category | flops | bytes accessed | tf_op | source)
XLA Modules:
  0.0 90.3 jit_solution(7947348766679554949)
XLA Ops:
  0.6 0.0 copy-start.5
  0.6 0.0 copy-start.6
  0.7 0.0 copy-start.7
  0.7 0.7 copy-done.5
  1.3 0.0 copy-done.6
  1.3 0.0 copy-done.7
  1.3 0.0 copy-start
  1.3 1.0 %copy-done = f32[1,8,16,1024]{3,2,1,0:T(8,128)S(1)} copy-done((f32[1,8,16,1024]{3,2,1,0:T(8,128)S(1)}, f32[1,8,16,1024]{3,2,1,0:T(8,128)}, u32[]{:S(2)}) %copy-start) | copy-done | bytes 524312
  2.4 0.0 copy-start.1
  2.4 1.0 %copy-done.1 = f32[3,8,8,512]{3,2,1,0:T(8,128)S(1)} copy-done((f32[3,8,8,512]{3,2,1,0:T(8,128)S(1)}, f32[3,8,8,512]{3,2,1,0:T(8,128)}, u32[]{:S(2)}) %copy-start.1) | copy-done | bytes 393240
  3.4 0.0 copy-start.2
  3.4 0.9 copy-done.2
  4.3 0.0 copy-start.3
  4.3 0.9 copy-done.3
  5.2 0.0 copy-start.4
  5.2 0.8 copy-done.4
  5.9 82.5 %calibrate.1 = (f32[64,64]{1,0:T(8,128)S(1)}, f32[64,64]{1,0:T(8,128)S(1)}, f32[192,64]{1,0:T(8,128)S(1)}) custom-call(s32[16]{0:T(128)S(1)} %bitcast.17, f32[8]{0:T(128)S(1)} %copy-done.7, f32[8,1024]{1,0:T(8,128)S(1)} %bitcast.14, f32[128,1024]{1,0:T(8,128)S(1)} %bitcast.9, s32[2,1024]{1,0:T(2,128)S(1)} %copy-done.5, f32[64,512]{1,0:T(8,128)S(1)} %bitcast.11, ...), custom_call_target="tpu_custom_call" | custom-call | tf_op jit(solution)/shard_map/calibrate/pallas_call | solution.py:549
  88.5 0.6 copy.14
  89.1 0.6 copy.15
  89.7 0.6 copy.16
Async XLA Ops:
  0.6 0.7 copy-start.5
  0.6 0.7 copy-start.6
  0.7 0.7 copy-start.7
  1.3 1.0 %copy-start = (f32[1,8,16,1024]{3,2,1,0:T(8,128)S(1)}, f32[1,8,16,1024]{3,2,1,0:T(8,128)}, u32[]{:S(2)}) copy-start(f32[1,8,16,1024]{3,2,1,0:T(8,128)} %param.9) | copy-start | bytes 1572868
  2.4 1.0 %copy-start.1 = (f32[3,8,8,512]{3,2,1,0:T(8,128)S(1)}, f32[3,8,8,512]{3,2,1,0:T(8,128)}, u32[]{:S(2)}) copy-start(f32[3,8,8,512]{3,2,1,0:T(8,128)} %param.13) | copy-start | bytes 1179652
  3.4 0.9 %copy-start.2 = (f32[1,8,8,512]{3,2,1,0:T(8,128)S(1)}, f32[1,8,8,512]{3,2,1,0:T(8,128)}, u32[]{:S(2)}) copy-start(f32[1,8,8,512]{3,2,1,0:T(8,128)} %param.12) | copy-start | bytes 393220
  4.3 0.9 %copy-start.3 = (f32[1,8,8,512]{3,2,1,0:T(8,128)S(1)}, f32[1,8,8,512]{3,2,1,0:T(8,128)}, u32[]{:S(2)}) copy-start(f32[1,8,8,512]{3,2,1,0:T(8,128)} %param.14) | copy-start | bytes 393220
  5.2 0.8 copy-start.4

commit v2 on v1

--- a/solution.py
+++ b/solution.py
@@ -144,9 +144,7 @@
     dual,
     anchor,
     e_src,
-    e_row,
-    e_stn,
-    e_chan,
+    e_all,
     sums_src,
     sums,
     gains_src,
@@ -172,18 +170,20 @@
     def chan_peer(d):
         return lax.rem(chan + d, chans)
 
+    everyone = chans * blocks
+    me = chan * blocks + stn
+
+    def any_peer(d):
+        peer = lax.rem(me + d, everyone)
+        return (lax.div(peer, blocks), lax.rem(peer, blocks))
+
     barrier = pltpu.get_barrier_semaphore()
 
-    def greet_stn(d, _):
-        pl.semaphore_signal(barrier, inc=1, device_id=(chan, stn_peer(d)), device_id_type=MESH)
+    def greet(d, _):
+        pl.semaphore_signal(barrier, inc=1, device_id=any_peer(d), device_id_type=MESH)
         return 0
 
-    def greet_chan(d, _):
-        pl.semaphore_signal(barrier, inc=1, device_id=(chan_peer(d), stn), device_id_type=MESH)
-        return 0
-
-    lax.fori_loop(1, blocks, greet_stn, 0)
-    lax.fori_loop(1, chans, greet_chan, 0)
+    lax.fori_loop(1, everyone, greet, 0)
 
     lane_start = pl.multiple_of(lax.div(stn, 2) * 128, 128)
     loads = [
@@ -273,7 +273,7 @@
         rho = jnp.where(k_row == k, rhos[k], rho)
     low_8 = low((8, 128))
 
-    pl.semaphore_wait(barrier, blocks + chans - 2)
+    pl.semaphore_wait(barrier, everyone - 1)
 
     def entries(ref, at):
         return [(ref[8 * i : 8 * i + 8, at], ref[32 + 8 * i : 40 + 8 * i, at]) for i in range(4)]
@@ -316,6 +316,20 @@
             return 0
 
         lax.fori_loop(1, chans, send, 0)
+
+    def to_all(src, dst, sem):
+        def send(d, _):
+            pltpu.make_async_remote_copy(
+                src_ref=src,
+                dst_ref=dst,
+                send_sem=sem.at[0],
+                recv_sem=sem.at[1],
+                device_id=any_peer(d),
+                device_id_type=MESH,
+            ).start()
+            return 0
+
+        lax.fori_loop(1, everyone, send, 0)
 
     def fit_of(step):
         wait_all(fits.at[step, pl.ds(0, chans - 1)], f_sem.at[step, 1])
@@ -385,8 +399,8 @@
 
         total = lax.fori_loop(0, chunks, residuals, jnp.zeros((1, WIDE), f32))
         e_src[it] = total
-        e_stn[it, stn] = total
-        to_stn(lambda _: e_src.at[it], e_stn.at[it, stn], e_sem.at[0, it])
+        e_all[it, me] = total
+        to_all(e_src.at[it], e_all.at[it, me], e_sem.at[it])
 
         def sums_of(i):
             at = chunk(i)
@@ -402,19 +416,9 @@
             sums_of(i)
             return 0
 
-        lax.fori_loop(0, chunks // 2, early, 0)
-        wait_all(e_stn.at[it, pl.ds(0, blocks - 1)], e_sem.at[0, it, 1])
-        total = e_stn[it, 0]
-        for n in range(1, blocks):
-            total = total + e_stn[it, n]
-        e_row[it] = total
-        e_chan[it, chan] = total
-        to_chan(e_row.at[it], e_chan.at[it, chan], e_sem.at[1, it])
-        lax.fori_loop(chunks // 2, chunks, early, 0)
-        wait_all(e_chan.at[it, pl.ds(0, chans - 1)], e_sem.at[1, it, 1])
-        total = e_chan[it, 0]
-        for n in range(1, chans):
-            total = total + e_chan[it, n]
+        lax.fori_loop(0, chunks, early, 0)
+        wait_all(e_all.at[it, pl.ds(0, chans * blocks - 1)], e_sem.at[it, 1])
+        total = jnp.sum(e_all[it], axis=0)
         noise = jnp.sum(total, axis=1, keepdims=True) * f32(1.0 / samples) + TINY
         scale = jnp.broadcast_to(1.0 / noise, (1, WIDE))
 
@@ -511,8 +515,7 @@
         fit_out[64 * t + 32 : 64 * t + 64, :] = swap(fit[t])[:, 0:64]
 
     def sent(it, _):
-        wait_all(e_stn.at[it, pl.ds(0, blocks - 1)], e_sem.at[0, it, 0])
-        wait_all(e_chan.at[it, pl.ds(0, chans - 1)], e_sem.at[1, it, 0])
+        wait_all(e_all.at[it, pl.ds(0, chans * blocks - 1)], e_sem.at[it, 0])
         wait_all(sums.at[it, pl.ds(0, blocks - 1)], s_sem.at[it, 0])
         return 0
 
@@ -540,7 +543,7 @@
         def run(*refs):
             kernel(chans, blocks, table, *refs)
 
-        any_spec = pl.BlockSpec(memory_space=pl.ANY)
+        any_spec = pl.BlockSpec(memory_space=pltpu.HBM)
         smem = pl.BlockSpec(memory_space=pltpu.SMEM)
         vmem = pl.BlockSpec(memory_space=pltpu.VMEM)
         dma = pltpu.SemaphoreType.DMA
@@ -582,9 +585,7 @@
                 state,
                 state,
                 pltpu.VMEM((PASSES, 1, 128), f32),
-                pltpu.VMEM((PASSES, 1, 128), f32),
-                pltpu.VMEM((PASSES, blocks, 1, 128), f32),
-                pltpu.VMEM((PASSES, chans, 1, 128), f32),
+                pltpu.VMEM((PASSES, chans * blocks, 1, 128), f32),
                 pltpu.VMEM((PASSES, blocks, 48, 128), f32),
                 pltpu.VMEM((PASSES, blocks, 48, 128), f32),
                 pltpu.VMEM((PASSES - 1, 32, 128), f32),
@@ -592,13 +593,13 @@
                 pltpu.VMEM((STEPS, 32, 128), f32),
                 pltpu.VMEM((STEPS, chans, 32, 128), f32),
                 dma((7,)),
-                dma((2, PASSES, 2)),
+                dma((PASSES, 2)),
                 dma((PASSES, 2)),
                 dma((PASSES - 1, 2)),
                 dma((STEPS, 2)),
             ],
             compiler_params=pltpu.CompilerParams(
-                collective_id=0, has_side_effects=True, vmem_limit_bytes=40 << 20
+                collective_id=0, has_side_effects=True, vmem_limit_bytes=62 << 20
             ),
             name="calibrate",
         )(

time: 90.7 us -> 85.3 us (0.940)
  local copies, waits for them, and re-layouts: 7.15 us -> 3.43 us
  Pallas kernels: 82.5 us -> 81 us
    unnamed x19 -> x5, local copies, waits for them, and re-layouts: 7.15 us -> 3.43 us
    pallas_call x1, Pallas kernels: 82.5 us -> 81 us  [body(): pl.pallas_call(run, out_shape=(jax.ShapeDtypeStruct((64, 64), f32), jax.S...]
where the time goes in v2:
time: 85.3 us; the launch traced here: 85.1 us
  Pallas kernels  81 us (95%)
  local copies, waits for them, and re-layouts  3.43 us (4%)
    pallas_call x1, Pallas kernels, body(): pl.pallas_call(run, out_shape=(jax.ShapeDtypeStruct((64, 64), f32), jax.S...  81 us
    unnamed x5, local copies, waits for them, and re-layouts  3.43 us

profile of v2, /device:TPU:1, one launch (start us, length us, event | category | flops | bytes accessed | tf_op | source)
XLA Modules:
  0.0 85.1 jit_solution(14196609563370320970)
XLA Ops:
  0.6 81.0 %calibrate.1 = (f32[64,64]{1,0:T(8,128)}, f32[64,64]{1,0:T(8,128)}, f32[192,64]{1,0:T(8,128)}) custom-call(s32[16]{0:T(128)} %bitcast.17, f32[8]{0:T(128)} %refs_1_.1, f32[8,1024]{1,0:T(8,128)} %bitcast.14, f32[128,1024]{1,0:T(8,128)} %bitcast.9, s32[2,1024]{1,0:T(2,128)} %refs_4_.1, f32[64,512]{1,0:T(8,128)} %bitcast.11, f32[192,512]{1,0:T(8,128)} %bitcast.10, ...), custom_call_target="tpu_custom_call" | custom-call | tf_op jit(solution)/shard_map/calibrate/pallas_call | solution.py:552
  81.7 0.0 copy-start
  81.7 1.4 %copy.14 = f32[1,8,8,64]{3,2,1,0:T(8,128)} copy(f32[1,8,8,64]{3,2,1,0:T(8,128)} %bitcast.16) | data formatting | bytes 32768
  83.1 1.4 %copy.15 = f32[1,8,8,64]{3,2,1,0:T(8,128)} copy(f32[1,8,8,64]{3,2,1,0:T(8,128)} %bitcast.15) | data formatting | bytes 32768
  84.5 0.0 copy-done
  84.5 0.6 copy.16
Async XLA Ops:
  81.7 2.8 %copy-start = (f32[192,64]{1,0:T(8,128)S(1)}, f32[192,64]{1,0:T(8,128)}, u32[]{:S(2)}) copy-start(f32[192,64]{1,0:T(8,128)} %get-tuple-element.8) | copy-start | bytes 147460

commit v3 on v2

v3 whole, which is shorter than its diff:
```python
import numpy as np
import jax
import jax.numpy as jnp
from jax import lax
from jax.experimental import pallas as pl
from jax.experimental.pallas import tpu as pltpu
from jax.sharding import PartitionSpec as P

PATHS = 8
SOURCES = 16
TERMS = 3
STEPS = 2
INNER = 2
PASSES = STEPS * INNER
NU = 2.0
TINY = 1e-06
LOGICAL = pl.DeviceIdType.LOGICAL
WIDE = 128
bf16 = jnp.bfloat16
f32 = jnp.float32


def basis_table(count):
    frequency = (2.0 * np.arange(count, dtype=np.float32) + 1.0) / np.float32(count) - 1.0
    columns = []
    for degree in range(TERMS):
        column = (frequency**degree).astype(np.float32)
        for earlier in columns:
            column = column - np.sum(earlier * column) / np.float32(count) * earlier
        column = column / np.sqrt(np.sum(column * column) / np.float32(count))
        columns.append(column.astype(np.float32))
    return np.stack(columns, axis=1)


def mul(a, b):
    return (a[0] * b[0] - a[1] * b[1], a[0] * b[1] + a[1] * b[0])


def mul_conj(a, b):
    return (a[0] * b[0] + a[1] * b[1], a[1] * b[0] - a[0] * b[1])


def conj_mul(a, b):
    return (a[0] * b[0] + a[1] * b[1], a[0] * b[1] - a[1] * b[0])


def add(a, b):
    return (a[0] + b[0], a[1] + b[1])


def product(a, b):
    return [
        add(mul(a[0], b[0]), mul(a[1], b[2])),
        add(mul(a[0], b[1]), mul(a[1], b[3])),
        add(mul(a[2], b[0]), mul(a[3], b[2])),
        add(mul(a[2], b[1]), mul(a[3], b[3])),
    ]


def product_with_adjoint(a, b):
    return [
        add(mul_conj(a[0], b[0]), mul_conj(a[1], b[1])),
        add(mul_conj(a[0], b[2]), mul_conj(a[1], b[3])),
        add(mul_conj(a[2], b[0]), mul_conj(a[3], b[1])),
        add(mul_conj(a[2], b[2]), mul_conj(a[3], b[3])),
    ]


def adjoint_product(a, b):
    return [
        add(conj_mul(a[0], b[0]), conj_mul(a[2], b[2])),
        add(conj_mul(a[0], b[1]), conj_mul(a[2], b[3])),
        add(conj_mul(a[1], b[0]), conj_mul(a[3], b[2])),
        add(conj_mul(a[1], b[1]), conj_mul(a[3], b[3])),
    ]


def power(a):
    return a[0] * a[0] + a[1] * a[1]


def gram(y):
    cross = add(mul_conj(y[0], y[2]), mul_conj(y[1], y[3]))
    return [power(y[0]) + power(y[1]), power(y[2]) + power(y[3]), cross[0], cross[1]]


def gram_of_adjoint(h):
    cross = add(conj_mul(h[0], h[1]), conj_mul(h[2], h[3]))
    return [power(h[0]) + power(h[2]), power(h[1]) + power(h[3]), cross[0], cross[1]]


def halves(x):
    top = x.astype(bf16)
    return top, (x - top.astype(f32)).astype(bf16)


def swap(x):
    return pltpu.roll(x, 64, 1)


def take(table, index):
    return jnp.take_along_axis(table, index, axis=1, mode="promise_in_bounds")


def masks_by_hops(everyone):
    hop = (0, 1, 2, 1)
    hops = lambda m: hop[m >> 1 & 3] + hop[m >> 3 & 3] + hop[m >> 5 & 3]
    return sorted(range(1, everyone), key=lambda m: (-hops(m), m))


SCRATCH = []


def scratch(name, *shape, dtype=f32):
    SCRATCH.append((name, pltpu.VMEM(shape, dtype)))


def lay_out(chans, blocks, baselines, stations):
    SCRATCH.clear()
    everyone = chans * blocks
    scratch("vis", 8, baselines)
    scratch("model", 8 * SOURCES, baselines)
    scratch("pairs", 2, baselines, dtype=jnp.int32)
    scratch("whole", 64 * stations // 128, 128)
    scratch("poly", 64 * TERMS * stations // 128, 128)
    scratch("dual_in", 64 * stations // 128, 128)
    scratch("coherent", 64, baselines)
    scratch("d_src", baselines // 128 * 64, 128)
    scratch("d_all", baselines // 128 * 64, 128)
    scratch("d_own", 64, baselines)
    scratch("pairs_all", blocks, 2, baselines, dtype=jnp.int32)
    scratch("index_p", blocks, baselines, dtype=jnp.int32)
    scratch("index_q", blocks, baselines, dtype=jnp.int32)
    scratch("table_q", 8 * stations // 128 * 8, 128)
    scratch("table_p", 64, 128)
    scratch("collect_p", blocks * 128, baselines, dtype=bf16)
    scratch("collect_q", blocks * 128, baselines, dtype=bf16)
    scratch("in_tile", blocks * 4 * 16, baselines, dtype=bf16)
    scratch("toward", 64, baselines)
    scratch("terms", 64, baselines)
    scratch("back", 64, baselines)
    scratch("parts_p", baselines // 128 * 16 * blocks, 128)
    scratch("parts_q", baselines // 128 * 16 * blocks, 128)
    scratch("weights", blocks, baselines)
    scratch("sums", 128, 128)
    scratch("gain", 64, 128)
    scratch("anchor", 64, 128)
    scratch("dual", stations // 16, 128)
    scratch("e_src", PASSES, 1, 128)
    scratch("e_all", PASSES, everyone, 1, 128)
    scratch("r_src", PASSES, baselines // 16, 128)
    scratch("r_all", PASSES, blocks * baselines // 16, 128)
    scratch("g_src", PASSES, stations // 16, 128)
    scratch("g_all", PASSES, blocks * stations // 16, 128)
    scratch("f_src", stations // 16, 128)
    scratch("f_all", chans, stations // 16, 128)
    scratch("s_src", blocks, 4, 128)
    scratch("s_all", everyone, 4, 128)
    scratch("j_src", blocks, 4, 128)
    scratch("j_all", blocks, 4, 128)
    scratch("unpack", 32, 128)
    dma = pltpu.SemaphoreType.DMA
    SCRATCH.append(("load_sem", dma((3 + 3 * stations // 128,))))
    for name, *shape in (
        ("p_sem", 2),
        ("d_sem", 2),
        ("e_sem", PASSES, 2),
        ("r_sem", PASSES, 2),
        ("g_sem", PASSES, 2),
        ("f_sem", 2),
        ("s_sem", 2),
        ("j_sem", 2),
    ):
        SCRATCH.append((name, dma(tuple(shape))))


class Held:
    def __init__(self, refs):
        for (name, _), ref in zip(SCRATCH, refs, strict=True):
            setattr(self, name, ref)


def kernel(
    chans,
    blocks,
    table,
    pointing,
    rhos,
    vis_hbm,
    model_hbm,
    pairs_hbm,
    gain_hbm,
    poly_hbm,
    dual_hbm,
    gain_out,
    dual_out,
    fit_out,
    *refs,
):
    v = Held(refs)
    stations = gain_hbm.shape[1]
    chan = lax.axis_index("chan")
    stn = lax.axis_index("stn")
    everyone = chans * blocks
    me = chan * blocks + stn
    baselines = v.vis.shape[1]
    tiles = stations // 128
    chunks = baselines // WIDE
    samples = float(everyone * baselines)

    flips = [(1 - 2 * lax.rem(lax.div(me, 1 << n), 2)) * (1 << n) for n in range(7)]

    def flipped(mask, start, count, base):
        for n in range(count):
            if mask >> n & 1:
                base = base + flips[start + n]
        return base

    uppers = [flipped(m, 4, 3, me) for m in range(8)]
    lowers = [flipped(m, 0, 4, 0) for m in range(16)]
    masks = masks_by_hops(everyone)

    def peer_of(mask):
        return uppers[mask >> 4] + lowers[mask & 15]

    stn_masks = [m for m in masks if m < blocks]
    chan_masks = [m for m in masks if m % blocks == 0]

    barrier = pltpu.get_barrier_semaphore()
    for mask in masks:
        pl.semaphore_signal(barrier, inc=1, device_id=peer_of(mask), device_id_type=LOGICAL)

    moves = [(model_hbm, v.model), (pairs_hbm, v.pairs), (vis_hbm, v.vis)]
    for src, dst in ((gain_hbm, v.whole), (dual_hbm, v.dual_in), (poly_hbm, v.poly)):
        rows = src.shape[0]
        moves += [
            (src.at[:, pl.ds(128 * j, 128)], dst.at[pl.ds(rows * j, rows)]) for j in range(tiles)
        ]
    loads = [pltpu.make_async_copy(a, b, v.load_sem.at[n]) for n, (a, b) in enumerate(moves)]
    for copy in loads:
        copy.start()

    def remote(src, dst, sem, peer):
        pltpu.make_async_remote_copy(
            src_ref=src,
            dst_ref=dst,
            send_sem=sem.at[0],
            recv_sem=sem.at[1],
            device_id=peer,
            device_id_type=LOGICAL,
        ).start()

    def to_stn(src, dst, sem):
        for mask in stn_masks:
            remote(src(stn + lowers[mask]), dst, sem, peer_of(mask))

    def wait_all(ref, sem):
        pltpu.make_async_copy(ref, ref, sem).wait()

    def chunk(i):
        return pl.ds(pl.multiple_of(i * WIDE, WIDE), WIDE)

    def entries(ref, at):
        return [(ref[8 * i : 8 * i + 8, at], ref[32 + 8 * i : 40 + 8 * i, at]) for i in range(4)]

    def keep(ref, at, values):
        for i in range(4):
            ref[8 * i : 8 * i + 8, at] = values[i][0]
            ref[32 + 8 * i : 40 + 8 * i, at] = values[i][1]

    def as_entries(values):
        return [(values[i], values[4 + i]) for i in range(4)]

    def picked(tile_of, index):
        within, tile = index & 127, index >> 7
        out = []
        for c in range(8):
            value = take(tile_of(c, 0), within)
            for j in range(1, tiles):
                value = jnp.where(tile == j, take(tile_of(c, j), within), value)
            out.append(value)
        return as_entries(out)

    lane = lax.broadcasted_iota(jnp.int32, (128, 128), 1)
    high = lax.broadcasted_iota(jnp.int32, (128, 128), 0)
    point = jnp.zeros((128, 128), jnp.int32)
    for s in range(SOURCES):
        point = jnp.where(lane % SOURCES == s, pointing[s], point)
    left, right = high % 64 // PATHS, high % PATHS
    component = jnp.where(high < 64, left, right)
    direction = jnp.where(high < 64, right, left)
    member = jnp.where((component == lane // SOURCES) & (direction == point), 1.0, 0.0).astype(bf16)
    loads[0].wait()

    def combine(i, _):
        at = pl.ds(pl.multiple_of(i * 256, 256), 256)
        m = v.model[:, at]
        m0 = m.astype(bf16)
        rest = m - m0.astype(f32)
        m1 = rest.astype(bf16)
        m2 = (rest - m1.astype(f32)).astype(bf16)
        both = (
            jnp.dot(member, m0, preferred_element_type=f32)
            + jnp.dot(member, m1, preferred_element_type=f32)
            + jnp.dot(member, m2, preferred_element_type=f32)
        )
        v.coherent[:, at] = both[0:64]
        for k in range(PATHS):
            for j in range(2):
                rows = pl.ds(pl.multiple_of(64 * k + 8 * (2 * i + j), 8), 8)
                v.d_src[rows] = both[64 + 8 * k : 72 + 8 * k, 128 * j : 128 * j + 128]
        return 0

    lax.fori_loop(0, baselines // 256, combine, 0)

    def mine(t):
        value = f32(0.0)
        for f in range(chans):
            value = jnp.where(chan == f, f32(table[f, t]), value)
        return value

    my_basis = [mine(t) for t in range(TERMS)]
    for copy in loads[1:]:
        copy.wait()

    def consensus_of(fit):
        value = my_basis[0] * fit[0]
        for t in range(1, TERMS):
            value = value + my_basis[t] * fit[t]
        return value

    def to_tiles(ref, rows):
        for j in range(tiles):
            ref[pl.ds(j, 8, stride=8), :] = rows[8 * j : 8 * j + 8]

    def own_of(ref, rows, start):
        return jnp.concatenate(
            [ref[pl.ds(rows * j + start + stn, 8, stride=8), :] for j in range(tiles)], axis=0
        )

    v.gain[...] = jnp.zeros((64, 128), f32)
    v.anchor[...] = jnp.zeros((64, 128), f32)
    v.sums[...] = jnp.zeros((128, 128), f32)
    to_tiles(v.gain, own_of(v.whole, 64, 0))
    dual_rows = own_of(v.dual_in, 64, 0)
    v.dual[...] = dual_rows
    to_tiles(v.anchor, consensus_of([own_of(v.poly, 64 * TERMS, 64 * t) for t in range(TERMS)]) - dual_rows)
    rho = rhos[stn]

    def keep_part(ref, i, n, value):
        ref[pl.ds(16 * blocks * i + n, blocks, stride=16), :] = value

    zeros = jnp.zeros((8, WIDE), f32)
    for n in range(12, 16):
        for i in range(chunks):
            keep_part(v.parts_p, i, n, zeros)
            keep_part(v.parts_q, i, n, zeros)
    sub = lax.broadcasted_iota(jnp.int32, (8, 128), 0)
    own_tile = pl.multiple_of(lax.div(stn, 2) * 64, 64)

    def spread_tables():
        rows = [v.gain[pl.ds(j, 8, stride=8), :] for j in range(tiles)]
        for c in range(8):
            per_block = None
            for j in range(tiles):
                value = jnp.broadcast_to(rows[j][c : c + 1], (8, 128))
                at = 8 * (c * tiles + j)
                v.table_q[at : at + 8, :] = value
                per_block = value if j == 0 else jnp.where(sub // 2 == j, value, per_block)
            v.table_p[8 * c : 8 * c + 8, :] = per_block

    def own_terms(i, _):
        at = chunk(i)
        d = entries(v.d_own, at)
        p = v.index_p[:, at]
        gain_p = as_entries([take(v.table_p[8 * c : 8 * c + 8, :], p) for c in range(8)])
        h = product(gain_p, d)
        keep(v.back, at, h)
        for n, part in enumerate(gram_of_adjoint(h)):
            keep_part(v.parts_q, i, n, part)

        def tile_of(c, j):
            return v.table_q[8 * (c * tiles + j) : 8 * (c * tiles + j) + 8, :]

        y = product_with_adjoint(d, picked(tile_of, v.index_q[:, at]))
        keep(v.toward, at, y)
        for n, part in enumerate(gram(y)):
            keep_part(v.parts_p, i, n, part)
        keep(v.terms, at, product(gain_p, y))
        return 0

    own_g, own_r = stations // 16, baselines // 16
    g_rows = pl.ds(pl.multiple_of(own_g * stn, own_g), own_g)
    r_rows = pl.ds(pl.multiple_of(own_r * stn, own_r), own_r)

    def one_pass(it, _):
        spread_tables()

        @pl.when(it > 0)
        def _():
            lax.fori_loop(0, chunks, own_terms, 0)
            wait_all(v.g_all.at[it - 1, pl.ds(0, (blocks - 1) * own_g)], v.g_sem.at[it - 1, 1])
            for j in range(tiles):
                for c in range(8):
                    v.whole[64 * j + 8 * c : 64 * j + 8 * c + 8] = v.g_all[
                        it - 1, pl.ds(8 * j + c, blocks, stride=own_g), :
                    ]

        def residuals(i, total):
            at = chunk(i)
            first = jnp.broadcast_to(v.pairs[0:1, at], (8, WIDE)) & 127
            second = jnp.broadcast_to(v.pairs[1:2, at], (8, WIDE))

            def tile_of(c, j):
                return v.whole[64 * j + 8 * c : 64 * j + 8 * c + 8]

            y = product_with_adjoint(entries(v.coherent, at), picked(tile_of, second))
            gain_p = as_entries(
                [take(v.whole[pl.ds(own_tile + 8 * c, 8)], first) for c in range(8)]
            )
            g = product(gain_p, y)
            e = None
            for n in range(4):
                for part in range(2):
                    c = n + 4 * part
                    left = v.vis[c : c + 1, at] - jnp.sum(g[n][part], axis=0, keepdims=True)
                    e = left * left if e is None else e + left * left
                    v.r_src[it, pl.ds(8 * i + c, 1)] = left
            return total + e

        total = lax.fori_loop(0, chunks, residuals, jnp.zeros((1, WIDE), f32))
        v.e_src[it] = total
        v.e_all[it, me] = total
        v.r_all[it, r_rows] = v.r_src[it]

        @pl.when(it == 0)
        def _():
            pl.semaphore_wait(barrier, everyone - 1)

        to_stn(lambda _: v.r_src.at[it], v.r_all.at[it, r_rows], v.r_sem.at[it])
        for mask in masks:
            remote(v.e_src.at[it], v.e_all.at[it, me], v.e_sem.at[it], peer_of(mask))

        @pl.when(it == 0)
        def _():
            to_stn(lambda _: v.pairs, v.pairs_all.at[stn], v.p_sem)
            to_stn(
                lambda peer: v.d_src.at[pl.ds(pl.multiple_of(own_r * peer, own_r), own_r)],
                v.d_all.at[r_rows],
                v.d_sem,
            )
            v.pairs_all[stn] = v.pairs[...]
            v.d_all[r_rows] = v.d_src[r_rows]
            wait_all(v.pairs_all.at[pl.ds(0, blocks - 1)], v.p_sem.at[1])
            row = lax.broadcasted_iota(jnp.int32, (128, baselines), 0)
            for i in range(blocks):
                first = v.pairs_all[i, 0:1, :]
                second = v.pairs_all[i, 1:2, :]
                v.index_p[i : i + 1, :] = first & 127
                v.index_q[i : i + 1, :] = second
                v.collect_p[128 * i : 128 * i + 128, :] = jnp.where(row == (first & 127), 1.0, 0.0).astype(bf16)
                v.collect_q[128 * i : 128 * i + 128, :] = jnp.where(row == (second & 127), 1.0, 0.0).astype(bf16)
                for j in range(tiles):
                    inside = jnp.where((second >> 7) == j, 1.0, 0.0)
                    at = 16 * (4 * i + j)
                    v.in_tile[at : at + 16, :] = jnp.broadcast_to(inside, (16, baselines)).astype(bf16)
            wait_all(v.d_all.at[pl.ds(0, (blocks - 1) * own_r)], v.d_sem.at[1])
            for i in range(chunks):
                at = slice(WIDE * i, WIDE * i + WIDE)
                for c in range(8):
                    v.d_own[8 * c : 8 * c + 8, at] = v.d_all[pl.ds(8 * i + c, blocks, stride=own_r), :]
            lax.fori_loop(0, chunks, own_terms, 0)

        wait_all(v.r_all.at[it, pl.ds(0, (blocks - 1) * own_r)], v.r_sem.at[it, 1])

        def products(i, _):
            at = chunk(i)
            y, h, g = entries(v.toward, at), entries(v.back, at), entries(v.terms, at)
            r = as_entries([v.r_all[it, pl.ds(8 * i + c, blocks, stride=own_r), :] for c in range(8)])
            v.weights[:, at] = power(r[0]) + power(r[1]) + power(r[2]) + power(r[3])
            x = [add(a, b) for a, b in zip(r, g)]
            b = product_with_adjoint(x, y)
            for n, part in enumerate([z[0] for z in b] + [z[1] for z in b]):
                keep_part(v.parts_p, i, 4 + n, part)
            b = adjoint_product(x, h)
            for n, part in enumerate([z[0] for z in b] + [z[1] for z in b]):
                keep_part(v.parts_q, i, 4 + n, part)
            return 0

        lax.fori_loop(0, chunks, products, 0)

        @pl.when(it == INNER)
        def _():
            wait_all(v.f_all.at[pl.ds(0, chans - 1)], v.f_sem.at[1])
            fit = [jnp.zeros((own_g, 128), f32)] * TERMS
            for f in range(chans):
                value = v.f_all[f]
                fit = [fit[t] + f32(table[f, t]) * value for t in range(TERMS)]
            consensus = consensus_of([z * f32(1.0 / chans) for z in fit])
            after = v.f_src[...] - consensus
            v.dual[...] = after
            to_tiles(v.anchor, consensus - after)

        wait_all(v.e_all.at[it, pl.ds(0, everyone - 1)], v.e_sem.at[it, 1])
        total = jnp.sum(v.e_all[it], axis=0)
        noise = jnp.sum(total, axis=1, keepdims=True) * f32(1.0 / samples) + TINY
        scale = jnp.broadcast_to(1.0 / noise, (1, 128))
        scale = jnp.concatenate([scale] * (baselines // 128), axis=1)
        v.weights[...] = (NU + 2.0) / (NU + v.weights[...] * scale)

        def collected(left, right):
            return lax.dot_general(left, right, (((1,), (1,)), ((), ())), preferred_element_type=f32)

        def block_of(ref, i):
            return jnp.concatenate(
                [ref[16 * (blocks * n + i) : 16 * (blocks * n + i) + 16, :] for n in range(chunks)], axis=1
            )

        got = [jnp.zeros((32, 128), f32) for _ in range(tiles)]
        for i in range(blocks):
            weight = v.weights[i : i + 1, :]
            wide = jnp.concatenate(halves(block_of(v.parts_p, i) * weight), axis=0)
            got[i // 2] = got[i // 2] + collected(wide, v.collect_p[128 * i : 128 * i + 128, :])
            top, rest = halves(block_of(v.parts_q, i) * weight)
            pieces = []
            for j in range(tiles):
                inside = v.in_tile[16 * (4 * i + j) : 16 * (4 * i + j) + 16, :]
                pieces += [top * inside, rest * inside]
            both = collected(jnp.concatenate(pieces, axis=0), v.collect_q[128 * i : 128 * i + 128, :])
            for j in range(tiles):
                got[j] = got[j] + both[32 * j : 32 * j + 32]
        for j in range(tiles):
            v.sums[pl.ds(j, 16, stride=8), :] = got[j][0:16] + got[j][16:32]

        def part(n):
            return v.sums[8 * n : 8 * n + 8, :]

        d1, d2, cr, ci = part(0) + rho, part(1) + rho, part(2), part(3)
        over = 1.0 / (d1 * d2 - cr * cr - ci * ci)
        right = as_entries([part(4 + n) + rho * v.anchor[8 * n : 8 * n + 8, :] for n in range(8)])
        up = (cr * over, ci * over)
        s1, s2 = d2 * over, d1 * over
        solved = []
        for r in range(2):
            x, y = right[2 * r], right[2 * r + 1]
            one = mul_conj(y, up)
            two = mul(x, up)
            solved.append((x[0] * s1 - one[0], x[1] * s1 - one[1]))
            solved.append((y[0] * s2 - two[0], y[1] * s2 - two[1]))
        for n in range(4):
            for k in range(2):
                at = 8 * (n + 4 * k)
                v.gain[at : at + 8, :] = 0.5 * (v.gain[at : at + 8, :] + solved[n][k])
        for j in range(tiles):
            v.g_src[it, 8 * j : 8 * j + 8, :] = v.gain[pl.ds(j, 8, stride=8), :]

        @pl.when(it < PASSES - 1)
        def _():
            to_stn(lambda _: v.g_src.at[it], v.g_all.at[it, g_rows], v.g_sem.at[it])
            v.g_all[it, g_rows] = v.g_src[it]

        @pl.when(it == INNER - 1)
        def _():
            v.f_src[...] = v.g_src[it] + v.dual[...]
            v.f_all[chan] = v.f_src[...]
            for mask in chan_masks:
                remote(v.f_src, v.f_all.at[chan], v.f_sem, peer_of(mask))

        return 0

    lax.fori_loop(0, PASSES, one_pass, 0)

    low = lax.broadcasted_iota(jnp.int32, (8, 128), 1) < 64

    def slices(ref, rows):
        for j in range(tiles):
            a = rows[8 * j : 8 * j + 8]
            under = pltpu.roll(a, 4, 0)
            ref[2 * j] = jnp.where(low, a, swap(under))[0:4]
            ref[2 * j + 1] = jnp.where(low, swap(a), under)[0:4]

    last = v.g_src[PASSES - 1]
    slices(v.s_src, last + v.dual[...])
    slices(v.j_src, last)
    for mask in masks:
        block = stn + lowers[mask & 7]
        remote(v.s_src.at[block], v.s_all.at[me], v.s_sem, peer_of(mask))
    to_stn(lambda peer: v.j_src.at[peer], v.j_all.at[stn], v.j_sem)
    v.s_all[me] = v.s_src[stn]
    v.j_all[stn] = v.j_src[stn]
    wait_all(v.j_all.at[pl.ds(0, blocks - 1)], v.j_sem.at[1])

    def give(ref, start, value):
        v.unpack[...] = value
        for n in range(4):
            rows = v.unpack[pl.ds(n, 8, stride=4), :]
            ref[start + 8 * n : start + 8 * n + 8, :] = rows[:, 0:64]
            ref[start + 32 + 8 * n : start + 40 + 8 * n, :] = swap(rows)[:, 0:64]

    give(gain_out, 0, v.j_all[...].reshape(32, 128))
    wait_all(v.s_all.at[pl.ds(0, everyone - 1)], v.s_sem.at[1])
    fit = [jnp.zeros((32, 128), f32)] * TERMS
    for f in range(chans):
        value = v.s_all[blocks * f : blocks * f + blocks].reshape(32, 128)
        fit = [fit[t] + f32(table[f, t]) * value for t in range(TERMS)]
    fit = [z * f32(1.0 / chans) for z in fit]
    for t in range(TERMS):
        give(fit_out, 64 * t, fit[t])
    give(dual_out, 0, v.s_all[pl.ds(blocks * chan, blocks)].reshape(32, 128) - consensus_of(fit))

    wait_all(v.pairs_all.at[pl.ds(0, blocks - 1)], v.p_sem.at[0])
    wait_all(v.d_all.at[pl.ds(0, (blocks - 1) * own_r)], v.d_sem.at[0])
    wait_all(v.f_all.at[pl.ds(0, chans - 1)], v.f_sem.at[0])
    wait_all(v.s_all.at[pl.ds(0, everyone - 1)], v.s_sem.at[0])
    wait_all(v.j_all.at[pl.ds(0, blocks - 1)], v.j_sem.at[0])
    for it in range(PASSES):
        wait_all(v.e_all.at[it, pl.ds(0, everyone - 1)], v.e_sem.at[it, 0])
        wait_all(v.r_all.at[it, pl.ds(0, (blocks - 1) * own_r)], v.r_sem.at[it, 0])
        if it < PASSES - 1:
            wait_all(v.g_all.at[it, pl.ds(0, (blocks - 1) * own_g)], v.g_sem.at[it, 0])


def solution(mesh):
    chans, blocks = mesh.shape["chan"], mesh.shape["stn"]
    table = basis_table(chans)

    def body(vis, model, pointing, pairs, gains, poly, dual, rhos):
        baselines = vis.shape[2]
        stations = gains.shape[3]

        def run(*refs):
            kernel(chans, blocks, table, *refs)

        any_spec = pl.BlockSpec(memory_space=pltpu.HBM)
        smem = pl.BlockSpec(memory_space=pltpu.SMEM)
        vmem = pl.BlockSpec(memory_space=pltpu.VMEM)
        lay_out(chans, blocks, baselines, stations)
        out = pl.pallas_call(
            run,
            out_shape=(
                jax.ShapeDtypeStruct((64, 64), f32),
                jax.ShapeDtypeStruct((64, 64), f32),
                jax.ShapeDtypeStruct((64 * TERMS, 64), f32),
            ),
            in_specs=[smem, smem] + [any_spec] * 6,
            out_specs=(vmem, vmem, vmem),
            scratch_shapes=[shape for _, shape in SCRATCH],
            compiler_params=pltpu.CompilerParams(
                collective_id=0, has_side_effects=True, vmem_limit_bytes=62 << 20
            ),
            name="calibrate",
        )(
            pointing.reshape(SOURCES),
            rhos,
            vis.reshape(8, baselines),
            model.reshape(8 * SOURCES, baselines),
            pairs,
            gains.reshape(64, stations),
            poly.reshape(64 * TERMS, stations),
            dual.reshape(64, stations),
        )
        return (
            out[0].reshape(1, 8, PATHS, 64),
            out[1].reshape(1, 8, PATHS, 64),
            out[2].reshape(TERMS, 8, PATHS, 64),
        )

    return jax.shard_map(
        body,
        mesh=mesh,
        in_specs=(
            P("chan", None, "stn"),
            P("chan", None, None, "stn"),
            P(),
            P(None, "stn"),
            P("chan", None, None, None),
            P(),
            P("chan", None, None, None),
            P(),
        ),
        out_specs=(
            P("chan", None, None, "stn"),
            P("chan", None, None, "stn"),
            P(None, None, None, "stn"),
        ),
        check_vma=False,
    )
```

time: 85.3 us -> 75.8 us (0.89)
  Pallas kernels: 81 us -> 71.5 us
    pallas_call x1, Pallas kernels: 81 us -> 71.5 us  [body(): pl.pallas_call(run, out_shape=(jax.ShapeDtypeStruct((64, 64), f32), jax.S...]
where the time goes in v3:
time: 75.8 us; the launch traced here: 75.5 us
  Pallas kernels  71.5 us (94%)
  local copies, waits for them, and re-layouts  3.43 us (5%)
    pallas_call x1, Pallas kernels, body(): pl.pallas_call(run, out_shape=(jax.ShapeDtypeStruct((64, 64), f32), jax.S...  71.5 us
    unnamed x5, local copies, waits for them, and re-layouts  3.43 us

profile of v3, /device:TPU:1, one launch (start us, length us, event | category | flops | bytes accessed | tf_op | source)
XLA Modules:
  0.0 75.5 jit_solution(11728491749226477193)
XLA Ops:
  0.6 71.5 %calibrate.1 = (f32[64,64]{1,0:T(8,128)}, f32[64,64]{1,0:T(8,128)}, f32[192,64]{1,0:T(8,128)}) custom-call(s32[16]{0:T(128)} %bitcast.17, f32[8]{0:T(128)} %refs_1_.1, f32[8,1024]{1,0:T(8,128)} %bitcast.14, f32[128,1024]{1,0:T(8,128)} %bitcast.9, s32[2,1024]{1,0:T(2,128)} %refs_4_.1, f32[64,512]{1,0:T(8,128)} %bitcast.11, f32[192,512]{1,0:T(8,128)} %bitcast.10, ...), custom_call_target="tpu_custom_call" | custom-call | tf_op jit(solution)/shard_map/calibrate/pallas_call | solution.py:638
  72.1 0.0 copy-start
  72.1 1.4 %copy.14 = f32[1,8,8,64]{3,2,1,0:T(8,128)} copy(f32[1,8,8,64]{3,2,1,0:T(8,128)} %bitcast.16) | data formatting | bytes 32768
  73.5 1.4 %copy.15 = f32[1,8,8,64]{3,2,1,0:T(8,128)} copy(f32[1,8,8,64]{3,2,1,0:T(8,128)} %bitcast.15) | data formatting | bytes 32768
  74.9 0.0 copy-done
  74.9 0.6 copy.16
Async XLA Ops:
  72.1 2.8 %copy-start = (f32[192,64]{1,0:T(8,128)S(1)}, f32[192,64]{1,0:T(8,128)}, u32[]{:S(2)}) copy-start(f32[192,64]{1,0:T(8,128)} %get-tuple-element.8) | copy-start | bytes 147460

commit v4 on v3

--- a/solution.py
+++ b/solution.py
@@ -133,8 +133,8 @@
     scratch("index_q", blocks, baselines, dtype=jnp.int32)
     scratch("table_q", 8 * stations // 128 * 8, 128)
     scratch("table_p", 64, 128)
-    scratch("collect_p", blocks * 128, baselines, dtype=bf16)
-    scratch("collect_q", blocks * 128, baselines, dtype=bf16)
+    scratch("collect", blocks * baselines, 256, dtype=bf16)
+    scratch("wide", 160, blocks * baselines, dtype=bf16)
     scratch("in_tile", blocks * 4 * 16, baselines, dtype=bf16)
     scratch("toward", 64, baselines)
     scratch("terms", 64, baselines)
@@ -158,7 +158,6 @@
     scratch("s_all", everyone, 4, 128)
     scratch("j_src", blocks, 4, 128)
     scratch("j_all", blocks, 4, 128)
-    scratch("unpack", 32, 128)
     dma = pltpu.SemaphoreType.DMA
     SCRATCH.append(("load_sem", dma((3 + 3 * stations // 128,))))
     for name, *shape in (
@@ -192,9 +191,7 @@
     gain_hbm,
     poly_hbm,
     dual_hbm,
-    gain_out,
-    dual_out,
-    fit_out,
+    packed,
     *refs,
 ):
     v = Held(refs)
@@ -398,7 +395,7 @@
 
         @pl.when(it > 0)
         def _():
-            lax.fori_loop(0, chunks, own_terms, 0)
+            lax.fori_loop(0, chunks, own_terms, 0, unroll=True)
             wait_all(v.g_all.at[it - 1, pl.ds(0, (blocks - 1) * own_g)], v.g_sem.at[it - 1, 1])
             for j in range(tiles):
                 for c in range(8):
@@ -428,7 +425,7 @@
                     v.r_src[it, pl.ds(8 * i + c, 1)] = left
             return total + e
 
-        total = lax.fori_loop(0, chunks, residuals, jnp.zeros((1, WIDE), f32))
+        total = lax.fori_loop(0, chunks, residuals, jnp.zeros((1, WIDE), f32), unroll=True)
         v.e_src[it] = total
         v.e_all[it, me] = total
         v.r_all[it, r_rows] = v.r_src[it]
@@ -436,30 +433,33 @@
         @pl.when(it == 0)
         def _():
             pl.semaphore_wait(barrier, everyone - 1)
-
-        to_stn(lambda _: v.r_src.at[it], v.r_all.at[it, r_rows], v.r_sem.at[it])
-        for mask in masks:
-            remote(v.e_src.at[it], v.e_all.at[it, me], v.e_sem.at[it], peer_of(mask))
-
-        @pl.when(it == 0)
-        def _():
             to_stn(lambda _: v.pairs, v.pairs_all.at[stn], v.p_sem)
             to_stn(
                 lambda peer: v.d_src.at[pl.ds(pl.multiple_of(own_r * peer, own_r), own_r)],
                 v.d_all.at[r_rows],
                 v.d_sem,
             )
+
+        to_stn(lambda _: v.r_src.at[it], v.r_all.at[it, r_rows], v.r_sem.at[it])
+        for mask in masks:
+            remote(v.e_src.at[it], v.e_all.at[it, me], v.e_sem.at[it], peer_of(mask))
+
+        @pl.when(it == 0)
+        def _():
             v.pairs_all[stn] = v.pairs[...]
             v.d_all[r_rows] = v.d_src[r_rows]
             wait_all(v.pairs_all.at[pl.ds(0, blocks - 1)], v.p_sem.at[1])
-            row = lax.broadcasted_iota(jnp.int32, (128, baselines), 0)
+            column = lax.broadcasted_iota(jnp.int32, (baselines, 128), 1).astype(f32)
             for i in range(blocks):
-                first = v.pairs_all[i, 0:1, :]
+                first = v.pairs_all[i, 0:1, :] & 127
                 second = v.pairs_all[i, 1:2, :]
-                v.index_p[i : i + 1, :] = first & 127
+                v.index_p[i : i + 1, :] = first
                 v.index_q[i : i + 1, :] = second
-                v.collect_p[128 * i : 128 * i + 128, :] = jnp.where(row == (first & 127), 1.0, 0.0).astype(bf16)
-                v.collect_q[128 * i : 128 * i + 128, :] = jnp.where(row == (second & 127), 1.0, 0.0).astype(bf16)
+                for start, index in ((0, second & 127), (128, first)):
+                    across = jnp.broadcast_to(index.astype(f32), (128, baselines)).T
+                    v.collect[baselines * i : baselines * i + baselines, start : start + 128] = jnp.where(
+                        column == across, 1.0, 0.0
+                    ).astype(bf16)
                 for j in range(tiles):
                     inside = jnp.where((second >> 7) == j, 1.0, 0.0)
                     at = 16 * (4 * i + j)
@@ -469,7 +469,7 @@
                 at = slice(WIDE * i, WIDE * i + WIDE)
                 for c in range(8):
                     v.d_own[8 * c : 8 * c + 8, at] = v.d_all[pl.ds(8 * i + c, blocks, stride=own_r), :]
-            lax.fori_loop(0, chunks, own_terms, 0)
+            lax.fori_loop(0, chunks, own_terms, 0, unroll=True)
 
         wait_all(v.r_all.at[it, pl.ds(0, (blocks - 1) * own_r)], v.r_sem.at[it, 1])
 
@@ -487,7 +487,7 @@
                 keep_part(v.parts_q, i, 4 + n, part)
             return 0
 
-        lax.fori_loop(0, chunks, products, 0)
+        lax.fori_loop(0, chunks, products, 0, unroll=True)
 
         @pl.when(it == INNER)
         def _():
@@ -508,27 +508,29 @@
         scale = jnp.concatenate([scale] * (baselines // 128), axis=1)
         v.weights[...] = (NU + 2.0) / (NU + v.weights[...] * scale)
 
-        def collected(left, right):
-            return lax.dot_general(left, right, (((1,), (1,)), ((), ())), preferred_element_type=f32)
-
         def block_of(ref, i):
             return jnp.concatenate(
                 [ref[16 * (blocks * n + i) : 16 * (blocks * n + i) + 16, :] for n in range(chunks)], axis=1
             )
 
-        got = [jnp.zeros((32, 128), f32) for _ in range(tiles)]
         for i in range(blocks):
             weight = v.weights[i : i + 1, :]
-            wide = jnp.concatenate(halves(block_of(v.parts_p, i) * weight), axis=0)
-            got[i // 2] = got[i // 2] + collected(wide, v.collect_p[128 * i : 128 * i + 128, :])
+            at = slice(baselines * i, baselines * i + baselines)
+            top, rest = halves(block_of(v.parts_p, i) * weight)
+            v.wide[128:144, at] = top
+            v.wide[144:160, at] = rest
             top, rest = halves(block_of(v.parts_q, i) * weight)
-            pieces = []
             for j in range(tiles):
                 inside = v.in_tile[16 * (4 * i + j) : 16 * (4 * i + j) + 16, :]
-                pieces += [top * inside, rest * inside]
-            both = collected(jnp.concatenate(pieces, axis=0), v.collect_q[128 * i : 128 * i + 128, :])
+                v.wide[32 * j : 32 * j + 16, at] = top * inside
+                v.wide[32 * j + 16 : 32 * j + 32, at] = rest * inside
+        got = [jnp.zeros((32, 128), f32) for _ in range(tiles)]
+        for n in range(8):
+            at = slice(1 * baselines * n, 1 * baselines * (n + 1))
+            every = jnp.dot(v.wide[:, at], v.collect[at, :], preferred_element_type=f32)
+            got[1 * n // 2] = got[1 * n // 2] + every[128:160, 128:256]
             for j in range(tiles):
-                got[j] = got[j] + both[32 * j : 32 * j + 32]
+                got[j] = got[j] + every[32 * j : 32 * j + 32, 0:128]
         for j in range(tiles):
             v.sums[pl.ds(j, 16, stride=8), :] = got[j][0:16] + got[j][16:32]
 
@@ -590,23 +592,16 @@
     v.j_all[stn] = v.j_src[stn]
     wait_all(v.j_all.at[pl.ds(0, blocks - 1)], v.j_sem.at[1])
 
-    def give(ref, start, value):
-        v.unpack[...] = value
-        for n in range(4):
-            rows = v.unpack[pl.ds(n, 8, stride=4), :]
-            ref[start + 8 * n : start + 8 * n + 8, :] = rows[:, 0:64]
-            ref[start + 32 + 8 * n : start + 40 + 8 * n, :] = swap(rows)[:, 0:64]
-
-    give(gain_out, 0, v.j_all[...].reshape(32, 128))
+    packed[0:32, :] = v.j_all[...].reshape(32, 128)
     wait_all(v.s_all.at[pl.ds(0, everyone - 1)], v.s_sem.at[1])
     fit = [jnp.zeros((32, 128), f32)] * TERMS
     for f in range(chans):
         value = v.s_all[blocks * f : blocks * f + blocks].reshape(32, 128)
         fit = [fit[t] + f32(table[f, t]) * value for t in range(TERMS)]
     fit = [z * f32(1.0 / chans) for z in fit]
+    packed[32:64, :] = v.s_all[pl.ds(blocks * chan, blocks)].reshape(32, 128) - consensus_of(fit)
     for t in range(TERMS):
-        give(fit_out, 64 * t, fit[t])
-    give(dual_out, 0, v.s_all[pl.ds(blocks * chan, blocks)].reshape(32, 128) - consensus_of(fit))
+        packed[64 + 32 * t : 96 + 32 * t, :] = fit[t]
 
     wait_all(v.pairs_all.at[pl.ds(0, blocks - 1)], v.p_sem.at[0])
     wait_all(v.d_all.at[pl.ds(0, (blocks - 1) * own_r)], v.d_sem.at[0])
@@ -620,6 +615,15 @@
             wait_all(v.g_all.at[it, pl.ds(0, (blocks - 1) * own_g)], v.g_sem.at[it, 0])
 
 
+def unpack(packed, gain_out, dual_out, fit_out):
+    spots = [(gain_out, 0), (dual_out, 0)] + [(fit_out, 64 * t) for t in range(TERMS)]
+    for m, (ref, start) in enumerate(spots):
+        for n in range(4):
+            rows = packed[pl.ds(32 * m + n, PATHS, stride=4), :]
+            ref[start + 8 * n : start + 8 * n + 8, :] = rows[:, 0:64]
+            ref[start + 32 + 8 * n : start + 40 + 8 * n, :] = swap(rows)[:, 0:64]
+
+
 def solution(mesh):
     chans, blocks = mesh.shape["chan"], mesh.shape["stn"]
     table = basis_table(chans)
@@ -635,15 +639,11 @@
         smem = pl.BlockSpec(memory_space=pltpu.SMEM)
         vmem = pl.BlockSpec(memory_space=pltpu.VMEM)
         lay_out(chans, blocks, baselines, stations)
-        out = pl.pallas_call(
+        packed = pl.pallas_call(
             run,
-            out_shape=(
-                jax.ShapeDtypeStruct((64, 64), f32),
-                jax.ShapeDtypeStruct((64, 64), f32),
-                jax.ShapeDtypeStruct((64 * TERMS, 64), f32),
-            ),
+            out_shape=jax.ShapeDtypeStruct((32 * (2 + TERMS), 128), f32),
             in_specs=[smem, smem] + [any_spec] * 6,
-            out_specs=(vmem, vmem, vmem),
+            out_specs=vmem,
             scratch_shapes=[shape for _, shape in SCRATCH],
             compiler_params=pltpu.CompilerParams(
                 collective_id=0, has_side_effects=True, vmem_limit_bytes=62 << 20
@@ -659,6 +659,18 @@
             poly.reshape(64 * TERMS, stations),
             dual.reshape(64, stations),
         )
+        out = pl.pallas_call(
+            unpack,
+            out_shape=(
+                jax.ShapeDtypeStruct((64, 64), f32),
+                jax.ShapeDtypeStruct((64, 64), f32),
+                jax.ShapeDtypeStruct((64 * TERMS, 64), f32),
+            ),
+            in_specs=[vmem],
+            out_specs=(vmem, vmem, vmem),
+            compiler_params=pltpu.CompilerParams(vmem_limit_bytes=62 << 20),
+            name="unpack",
+        )(packed)
         return (
             out[0].reshape(1, 8, PATHS, 64),
             out[1].reshape(1, 8, PATHS, 64),

time: 75.8 us -> 68.2 us (0.90)
  Pallas kernels: 71.5 us -> 67.3 us
  local copies, waits for them, and re-layouts: 3.43 us -> 0 us
    pallas_call x1 -> x2, Pallas kernels: 71.5 us -> 67.3 us  [the longest x1 65.7 us: body(): pl.pallas_call(run, out_shape=jax.ShapeDtypeStruct((32 * (2 + TERMS), 128...]
    unnamed x5 -> x0, local copies, waits for them, and re-layouts: 3.43 us -> none
where the time goes in v4:
time: 68.2 us; the launch traced here: 68 us
  Pallas kernels  67.3 us (99%)
    pallas_call x1, Pallas kernels, body(): pl.pallas_call(run, out_shape=jax.ShapeDtypeStruct((32 * (2 + TERMS), 128...  65.7 us
    pallas_call x1, Pallas kernels, body(): pl.pallas_call(unpack, out_shape=(jax.ShapeDtypeStruct((64, 64), f32), ja...  1.62 us

profile of v4, /device:TPU:1, one launch (start us, length us, event | category | flops | bytes accessed | tf_op | source)
XLA Modules:
  0.0 68.0 jit_solution(7485105279886367546)
XLA Ops:
  0.6 65.7 %calibrate.1.packed = f32[160,128]{1,0:T(8,128)} custom-call(s32[16]{0:T(128)} %bitcast.14, f32[8]{0:T(128)} %refs_1_.1, f32[8,1024]{1,0:T(8,128)} %bitcast.13, f32[128,1024]{1,0:T(8,128)} %bitcast.9, s32[2,1024]{1,0:T(2,128)} %refs_4_.1, f32[64,512]{1,0:T(8,128)} %bitcast.11, f32[192,512]{1,0:T(8,128)} %bitcast.10, f32[64,512]{1,0:T(8,128)} %bitcast.12), custom_call_target="tpu_custom_call" | custom-call | tf_op jit(solution)/shard_map/calibrate/pallas_call | solution.py:642
  66.4 1.6 %unpack.1 = (f32[64,64]{1,0:T(8,128)}, f32[64,64]{1,0:T(8,128)}, f32[192,64]{1,0:T(8,128)}) custom-call(f32[160,128]{1,0:T(8,128)} %calibrate.1.packed), custom_call_target="tpu_custom_call" | custom-call | tf_op jit(solution)/shard_map/unpack/pallas_call | solution.py:662

commit v5 on v4

--- a/solution.py
+++ b/solution.py
@@ -134,7 +134,6 @@
     scratch("table_q", 8 * stations // 128 * 8, 128)
     scratch("table_p", 64, 128)
     scratch("collect", blocks * baselines, 256, dtype=bf16)
-    scratch("wide", 160, blocks * baselines, dtype=bf16)
     scratch("in_tile", blocks * 4 * 16, baselines, dtype=bf16)
     scratch("toward", 64, baselines)
     scratch("terms", 64, baselines)
@@ -146,8 +145,8 @@
     scratch("gain", 64, 128)
     scratch("anchor", 64, 128)
     scratch("dual", stations // 16, 128)
-    scratch("e_src", PASSES, 1, 128)
-    scratch("e_all", PASSES, everyone, 1, 128)
+    scratch("e_src", PASSES, 8, 128)
+    scratch("e_all", PASSES, everyone, 128)
     scratch("r_src", PASSES, baselines // 16, 128)
     scratch("r_all", PASSES, blocks * baselines // 16, 128)
     scratch("g_src", PASSES, stations // 16, 128)
@@ -164,7 +163,7 @@
         ("p_sem", 2),
         ("d_sem", 2),
         ("e_sem", PASSES, 2),
-        ("r_sem", PASSES, 2),
+        ("r_sem", PASSES, 3),
         ("g_sem", PASSES, 2),
         ("f_sem", 2),
         ("s_sem", 2),
@@ -251,6 +250,16 @@
         for mask in stn_masks:
             remote(src(stn + lowers[mask]), dst, sem, peer_of(mask))
 
+    def to_partner(src, dst, sem):
+        pltpu.make_async_remote_copy(
+            src_ref=src,
+            dst_ref=dst,
+            send_sem=sem.at[0],
+            recv_sem=sem.at[2],
+            device_id=peer_of(1),
+            device_id_type=LOGICAL,
+        ).start()
+
     def wait_all(ref, sem):
         pltpu.make_async_copy(ref, ref, sem).wait()
 
@@ -289,26 +298,27 @@
     member = jnp.where((component == lane // SOURCES) & (direction == point), 1.0, 0.0).astype(bf16)
     loads[0].wait()
 
-    def combine(i, _):
-        at = pl.ds(pl.multiple_of(i * 256, 256), 256)
-        m = v.model[:, at]
-        m0 = m.astype(bf16)
-        rest = m - m0.astype(f32)
-        m1 = rest.astype(bf16)
-        m2 = (rest - m1.astype(f32)).astype(bf16)
-        both = (
-            jnp.dot(member, m0, preferred_element_type=f32)
-            + jnp.dot(member, m1, preferred_element_type=f32)
-            + jnp.dot(member, m2, preferred_element_type=f32)
-        )
-        v.coherent[:, at] = both[0:64]
-        for k in range(PATHS):
-            for j in range(2):
-                rows = pl.ds(pl.multiple_of(64 * k + 8 * (2 * i + j), 8), 8)
-                v.d_src[rows] = both[64 + 8 * k : 72 + 8 * k, 128 * j : 128 * j + 128]
-        return 0
-
-    lax.fori_loop(0, baselines // 256, combine, 0)
+    def combine(*accs):
+        twice = jnp.concatenate([member, member], axis=1)
+        for i in range(baselines // 256):
+            m = v.model[:, 256 * i : 256 * i + 256]
+            m0 = m.astype(bf16)
+            rest = m - m0.astype(f32)
+            m1 = rest.astype(bf16)
+            m2 = (rest - m1.astype(f32)).astype(bf16)
+            two = jnp.concatenate([m0, m1], axis=0)
+            one = jnp.concatenate([m2, jnp.zeros((128, 256), bf16)], axis=0)
+            for n, part in enumerate((two, one)):
+                pltpu.matmul_push_rhs(part, staging_register=n, mxu_index=i % 2)
+                pltpu.matmul_acc_lhs(accs[i % 2], twice, load_staged_rhs=n)
+            both = pltpu.matmul_pop(accs[i % 2])
+            v.coherent[:, 256 * i : 256 * i + 256] = both[0:64]
+            for k in range(PATHS):
+                for j in range(2):
+                    row = 64 * k + 8 * (2 * i + j)
+                    v.d_src[row : row + 8] = both[64 + 8 * k : 72 + 8 * k, 128 * j : 128 * j + 128]
+
+    pl.run_scoped(combine, *[pltpu.ACC(m)((128, 256), f32) for m in range(2)])
 
     def mine(t):
         value = f32(0.0)
@@ -389,6 +399,14 @@
     own_g, own_r = stations // 16, baselines // 16
     g_rows = pl.ds(pl.multiple_of(own_g * stn, own_g), own_g)
     r_rows = pl.ds(pl.multiple_of(own_r * stn, own_r), own_r)
+
+    def pass_on(it):
+        wait_all(v.r_all.at[it, pl.ds(0, (blocks // 2 - 1) * own_r)], v.r_sem.at[it, 1])
+        for mask in stn_masks:
+            if mask % 2 == 0:
+                start = pl.multiple_of(own_r * (stn + lowers[mask]), own_r)
+                rows = v.r_all.at[it, pl.ds(start, own_r)]
+                to_partner(rows, rows, v.r_sem.at[it])
 
     def one_pass(it, _):
         spread_tables()
@@ -426,8 +444,8 @@
             return total + e
 
         total = lax.fori_loop(0, chunks, residuals, jnp.zeros((1, WIDE), f32), unroll=True)
-        v.e_src[it] = total
-        v.e_all[it, me] = total
+        v.e_src[it, 0:1] = total
+        v.e_all[it, pl.ds(me, 1)] = total
         v.r_all[it, r_rows] = v.r_src[it]
 
         @pl.when(it == 0)
@@ -440,9 +458,12 @@
                 v.d_sem,
             )
 
-        to_stn(lambda _: v.r_src.at[it], v.r_all.at[it, r_rows], v.r_sem.at[it])
+        for mask in stn_masks:
+            if mask % 2 == 0:
+                remote(v.r_src.at[it], v.r_all.at[it, r_rows], v.r_sem.at[it], peer_of(mask))
+        to_partner(v.r_src.at[it], v.r_all.at[it, r_rows], v.r_sem.at[it])
         for mask in masks:
-            remote(v.e_src.at[it], v.e_all.at[it, me], v.e_sem.at[it], peer_of(mask))
+            remote(v.e_src.at[it, pl.ds(0, 1)], v.e_all.at[it, pl.ds(me, 1)], v.e_sem.at[it], peer_of(mask))
 
         @pl.when(it == 0)
         def _():
@@ -469,9 +490,14 @@
                 at = slice(WIDE * i, WIDE * i + WIDE)
                 for c in range(8):
                     v.d_own[8 * c : 8 * c + 8, at] = v.d_all[pl.ds(8 * i + c, blocks, stride=own_r), :]
+            pass_on(it)
             lax.fori_loop(0, chunks, own_terms, 0, unroll=True)
 
-        wait_all(v.r_all.at[it, pl.ds(0, (blocks - 1) * own_r)], v.r_sem.at[it, 1])
+        @pl.when(it > 0)
+        def _():
+            pass_on(it)
+
+        wait_all(v.r_all.at[it, pl.ds(0, blocks // 2 * own_r)], v.r_sem.at[it, 2])
 
         def products(i, _):
             at = chunk(i)
@@ -502,37 +528,45 @@
             to_tiles(v.anchor, consensus - after)
 
         wait_all(v.e_all.at[it, pl.ds(0, everyone - 1)], v.e_sem.at[it, 1])
-        total = jnp.sum(v.e_all[it], axis=0)
+        total = jnp.sum(v.e_all[it], axis=0, keepdims=True)
         noise = jnp.sum(total, axis=1, keepdims=True) * f32(1.0 / samples) + TINY
         scale = jnp.broadcast_to(1.0 / noise, (1, 128))
         scale = jnp.concatenate([scale] * (baselines // 128), axis=1)
         v.weights[...] = (NU + 2.0) / (NU + v.weights[...] * scale)
 
-        def block_of(ref, i):
-            return jnp.concatenate(
-                [ref[16 * (blocks * n + i) : 16 * (blocks * n + i) + 16, :] for n in range(chunks)], axis=1
-            )
-
-        for i in range(blocks):
-            weight = v.weights[i : i + 1, :]
-            at = slice(baselines * i, baselines * i + baselines)
-            top, rest = halves(block_of(v.parts_p, i) * weight)
-            v.wide[128:144, at] = top
-            v.wide[144:160, at] = rest
-            top, rest = halves(block_of(v.parts_q, i) * weight)
+        def block_of(ref, i, start):
+            rows = [16 * (blocks * n + i) for n in range(start // 128, start // 128 + 2)]
+            return jnp.concatenate([ref[row : row + 16, :] for row in rows], axis=1)
+
+        def accumulate(*accs):
+            acc_q, acc_p = accs[:2], (accs[2 : 2 + tiles], accs[2 + tiles :])
+            for step in range(blocks * baselines // 512):
+                for m in range(2):
+                    i = 2 * (step * 256 // baselines) + m
+                    start = baselines * i + step * 256 % baselines
+                    at = slice(start, start + 256)
+                    pltpu.matmul_push_rhs(v.collect[at, :], staging_register=step % 2, mxu_index=m)
+                    here = slice(start - baselines * i, start - baselines * i + 256)
+                    weight = v.weights[i : i + 1, here]
+                    top, rest = halves(block_of(v.parts_q, i, here.start) * weight)
+                    pieces = []
+                    for j in range(tiles):
+                        inside = v.in_tile[16 * (4 * i + j) : 16 * (4 * i + j) + 16, here]
+                        pieces += [top * inside, rest * inside]
+                    pltpu.matmul_acc_lhs(
+                        acc_q[m], jnp.concatenate(pieces, axis=0), load_staged_rhs=step % 2
+                    )
+                    pieces = halves(block_of(v.parts_p, i, here.start) * weight)
+                    pltpu.matmul_acc_lhs(acc_p[m][i // 2], jnp.concatenate(pieces, axis=0))
+            every = pltpu.matmul_pop(acc_q[0]) + pltpu.matmul_pop(acc_q[1])
             for j in range(tiles):
-                inside = v.in_tile[16 * (4 * i + j) : 16 * (4 * i + j) + 16, :]
-                v.wide[32 * j : 32 * j + 16, at] = top * inside
-                v.wide[32 * j + 16 : 32 * j + 32, at] = rest * inside
-        got = [jnp.zeros((32, 128), f32) for _ in range(tiles)]
-        for n in range(8):
-            at = slice(1 * baselines * n, 1 * baselines * (n + 1))
-            every = jnp.dot(v.wide[:, at], v.collect[at, :], preferred_element_type=f32)
-            got[1 * n // 2] = got[1 * n // 2] + every[128:160, 128:256]
-            for j in range(tiles):
-                got[j] = got[j] + every[32 * j : 32 * j + 32, 0:128]
-        for j in range(tiles):
-            v.sums[pl.ds(j, 16, stride=8), :] = got[j][0:16] + got[j][16:32]
+                here = pltpu.matmul_pop(acc_p[0][j]) + pltpu.matmul_pop(acc_p[1][j])
+                got = every[32 * j : 32 * j + 32, 0:128] + here[:, 128:256]
+                v.sums[pl.ds(j, 16, stride=8), :] = got[0:16] + got[16:32]
+
+        accs = [pltpu.ACC(m)((128, 256), f32) for m in range(2)]
+        accs += [pltpu.ACC(m)((32, 256), f32) for m in range(2) for _ in range(tiles)]
+        pl.run_scoped(accumulate, *accs)
 
         def part(n):
             return v.sums[8 * n : 8 * n + 8, :]
@@ -627,6 +661,7 @@
 def solution(mesh):
     chans, blocks = mesh.shape["chan"], mesh.shape["stn"]
     table = basis_table(chans)
+    abstract = mesh.abstract_mesh
 
     def body(vis, model, pointing, pairs, gains, poly, dual, rhos):
         baselines = vis.shape[2]
@@ -635,10 +670,10 @@
         def run(*refs):
             kernel(chans, blocks, table, *refs)
 
+        lay_out(chans, blocks, baselines, stations)
         any_spec = pl.BlockSpec(memory_space=pltpu.HBM)
         smem = pl.BlockSpec(memory_space=pltpu.SMEM)
         vmem = pl.BlockSpec(memory_space=pltpu.VMEM)
-        lay_out(chans, blocks, baselines, stations)
         packed = pl.pallas_call(
             run,
             out_shape=jax.ShapeDtypeStruct((32 * (2 + TERMS), 128), f32),

time: 68.2 us -> 66.4 us (0.974)
  Pallas kernels: 67.3 us -> 65.6 us
    pallas_call x1, Pallas kernels: 65.7 us -> 63.9 us  [body(): pl.pallas_call(run, out_shape=jax.ShapeDtypeStruct((32 * (2 + TERMS), 128...]
where the time goes in v5:
time: 66.4 us; the launch traced here: 66.2 us
  Pallas kernels  65.6 us (99%)
    pallas_call x1, Pallas kernels, body(): pl.pallas_call(run, out_shape=jax.ShapeDtypeStruct((32 * (2 + TERMS), 128...  63.9 us
    pallas_call x1, Pallas kernels, body(): pl.pallas_call(unpack, out_shape=(jax.ShapeDtypeStruct((64, 64), f32), ja...  1.62 us

profile of v5, /device:TPU:1, one launch (start us, length us, event | category | flops | bytes accessed | tf_op | source)
XLA Modules:
  0.0 66.2 jit_solution(6098849714060942218)
XLA Ops:
  0.6 63.9 %calibrate.1.packed = f32[160,128]{1,0:T(8,128)} custom-call(s32[16]{0:T(128)} %bitcast.14, f32[8]{0:T(128)} %refs_1_.1, f32[8,1024]{1,0:T(8,128)} %bitcast.13, f32[128,1024]{1,0:T(8,128)} %bitcast.9, s32[2,1024]{1,0:T(2,128)} %refs_4_.1, f32[64,512]{1,0:T(8,128)} %bitcast.11, f32[192,512]{1,0:T(8,128)} %bitcast.10, f32[64,512]{1,0:T(8,128)} %bitcast.12), custom_call_target="tpu_custom_call" | custom-call | tf_op jit(solution)/shard_map/calibrate/pallas_call | solution.py:677
  64.6 1.6 %unpack.1 = (f32[64,64]{1,0:T(8,128)}, f32[64,64]{1,0:T(8,128)}, f32[192,64]{1,0:T(8,128)}) custom-call(f32[160,128]{1,0:T(8,128)} %calibrate.1.packed), custom_call_target="tpu_custom_call" | custom-call | tf_op jit(solution)/shard_map/unpack/pallas_call | solution.py:697

commit v6 on v5

--- a/solution.py
+++ b/solution.py
@@ -157,8 +157,10 @@
     scratch("s_all", everyone, 4, 128)
     scratch("j_src", blocks, 4, 128)
     scratch("j_all", blocks, 4, 128)
+    SCRATCH.append(("pointing", pltpu.SMEM((SOURCES,), jnp.int32)))
+    SCRATCH.append(("rhos", pltpu.SMEM((PATHS,), f32)))
     dma = pltpu.SemaphoreType.DMA
-    SCRATCH.append(("load_sem", dma((3 + 3 * stations // 128,))))
+    SCRATCH.append(("load_sem", dma((5 + 3 * stations // 128,))))
     for name, *shape in (
         ("p_sem", 2),
         ("d_sem", 2),
@@ -182,8 +184,8 @@
     chans,
     blocks,
     table,
-    pointing,
-    rhos,
+    pointing_hbm,
+    rhos_hbm,
     vis_hbm,
     model_hbm,
     pairs_hbm,
@@ -226,7 +228,9 @@
     for mask in masks:
         pl.semaphore_signal(barrier, inc=1, device_id=peer_of(mask), device_id_type=LOGICAL)
 
-    moves = [(model_hbm, v.model), (pairs_hbm, v.pairs), (vis_hbm, v.vis)]
+    pointing, rhos = v.pointing, v.rhos
+    moves = [(pointing_hbm, pointing), (rhos_hbm, rhos), (model_hbm, v.model)]
+    moves += [(pairs_hbm, v.pairs), (vis_hbm, v.vis)]
     for src, dst in ((gain_hbm, v.whole), (dual_hbm, v.dual_in), (poly_hbm, v.poly)):
         rows = src.shape[0]
         moves += [
@@ -287,6 +291,9 @@
             out.append(value)
         return as_entries(out)
 
+    loads[0].wait()
+    loads[1].wait()
+
     lane = lax.broadcasted_iota(jnp.int32, (128, 128), 1)
     high = lax.broadcasted_iota(jnp.int32, (128, 128), 0)
     point = jnp.zeros((128, 128), jnp.int32)
@@ -296,7 +303,7 @@
     component = jnp.where(high < 64, left, right)
     direction = jnp.where(high < 64, right, left)
     member = jnp.where((component == lane // SOURCES) & (direction == point), 1.0, 0.0).astype(bf16)
-    loads[0].wait()
+    loads[2].wait()
 
     def combine(*accs):
         twice = jnp.concatenate([member, member], axis=1)
@@ -327,7 +334,7 @@
         return value
 
     my_basis = [mine(t) for t in range(TERMS)]
-    for copy in loads[1:]:
+    for copy in loads[3:]:
         copy.wait()
 
     def consensus_of(fit):
@@ -452,11 +459,6 @@
         def _():
             pl.semaphore_wait(barrier, everyone - 1)
             to_stn(lambda _: v.pairs, v.pairs_all.at[stn], v.p_sem)
-            to_stn(
-                lambda peer: v.d_src.at[pl.ds(pl.multiple_of(own_r * peer, own_r), own_r)],
-                v.d_all.at[r_rows],
-                v.d_sem,
-            )
 
         for mask in stn_masks:
             if mask % 2 == 0:
@@ -467,6 +469,11 @@
 
         @pl.when(it == 0)
         def _():
+            to_stn(
+                lambda peer: v.d_src.at[pl.ds(pl.multiple_of(own_r * peer, own_r), own_r)],
+                v.d_all.at[r_rows],
+                v.d_sem,
+            )
             v.pairs_all[stn] = v.pairs[...]
             v.d_all[r_rows] = v.d_src[r_rows]
             wait_all(v.pairs_all.at[pl.ds(0, blocks - 1)], v.p_sem.at[1])
@@ -672,27 +679,26 @@
 
         lay_out(chans, blocks, baselines, stations)
         any_spec = pl.BlockSpec(memory_space=pltpu.HBM)
-        smem = pl.BlockSpec(memory_space=pltpu.SMEM)
         vmem = pl.BlockSpec(memory_space=pltpu.VMEM)
         packed = pl.pallas_call(
             run,
             out_shape=jax.ShapeDtypeStruct((32 * (2 + TERMS), 128), f32),
-            in_specs=[smem, smem] + [any_spec] * 6,
+            in_specs=[any_spec] * 8,
             out_specs=vmem,
             scratch_shapes=[shape for _, shape in SCRATCH],
             compiler_params=pltpu.CompilerParams(
-                collective_id=0, has_side_effects=True, vmem_limit_bytes=62 << 20
+                collective_id=0, has_side_effects=True, vmem_limit_bytes=40 << 20
             ),
             name="calibrate",
         )(
-            pointing.reshape(SOURCES),
-            rhos,
-            vis.reshape(8, baselines),
-            model.reshape(8 * SOURCES, baselines),
-            pairs,
-            gains.reshape(64, stations),
-            poly.reshape(64 * TERMS, stations),
-            dual.reshape(64, stations),
+            pltpu.with_memory_space_constraint(pointing.reshape(SOURCES), pltpu.HBM),
+            pltpu.with_memory_space_constraint(rhos, pltpu.HBM),
+            pltpu.with_memory_space_constraint(vis.reshape(8, baselines), pltpu.HBM),
+            pltpu.with_memory_space_constraint(model.reshape(8 * SOURCES, baselines), pltpu.HBM),
+            pltpu.with_memory_space_constraint(pairs, pltpu.HBM),
+            pltpu.with_memory_space_constraint(gains.reshape(64, stations), pltpu.HBM),
+            pltpu.with_memory_space_constraint(poly.reshape(64 * TERMS, stations), pltpu.HBM),
+            pltpu.with_memory_space_constraint(dual.reshape(64, stations), pltpu.HBM),
         )
         out = pl.pallas_call(
             unpack,
@@ -703,7 +709,7 @@
             ),
             in_specs=[vmem],
             out_specs=(vmem, vmem, vmem),
-            compiler_params=pltpu.CompilerParams(vmem_limit_bytes=62 << 20),
+            compiler_params=pltpu.CompilerParams(vmem_limit_bytes=16 << 20),
             name="unpack",
         )(packed)
         return (

time: 66.4 us -> 63.5 us (0.956)
  Pallas kernels: 65.6 us -> 62.7 us
    pallas_call x1, Pallas kernels: 63.9 us -> 62 us  [body(): pl.pallas_call(run, out_shape=jax.ShapeDtypeStruct((32 * (2 + TERMS), 128...]
    pallas_call x1, Pallas kernels: 1.62 us -> 0.73 us  [body(): pl.pallas_call(unpack, out_shape=(jax.ShapeDtypeStruct((64, 64), f32), ja...]
where the time goes in v6:
time: 63.5 us; the launch traced here: 63.4 us
  Pallas kernels  62.7 us (99%)
  between operations  0.64 us (1%)
    pallas_call x1, Pallas kernels, body(): pl.pallas_call(run, out_shape=jax.ShapeDtypeStruct((32 * (2 + TERMS), 128...  62 us

profile of v6, /device:TPU:1, one launch (start us, length us, event | category | flops | bytes accessed | tf_op | source)
XLA Modules:
  0.0 63.4 jit_solution(3921895716572480692)
XLA Ops:
  0.6 62.0 %calibrate.1.packed = f32[160,128]{1,0:T(8,128)S(1)} custom-call(s32[16]{0:T(128)} %bitcast.14, f32[8]{0:T(128)} %refs_1_.1, f32[8,1024]{1,0:T(8,128)} %bitcast.13, f32[128,1024]{1,0:T(8,128)} %bitcast.9, s32[2,1024]{1,0:T(2,128)} %refs_4_.1, f32[64,512]{1,0:T(8,128)} %bitcast.11, f32[192,512]{1,0:T(8,128)} %bitcast.10, f32[64,512]{1,0:T(8,128)} %bitcast.12), custom_call_target="tpu_custom_call" | custom-call | tf_op jit(solution)/shard_map/calibrate/pallas_call | solution.py:683
  62.6 0.7 %unpack.1 = (f32[64,64]{1,0:T(8,128)}, f32[64,64]{1,0:T(8,128)}, f32[192,64]{1,0:T(8,128)}) custom-call(f32[160,128]{1,0:T(8,128)S(1)} %calibrate.1.packed), custom_call_target="tpu_custom_call" | custom-call | tf_op jit(solution)/shard_map/unpack/pallas_call | solution.py:703

commit v7 on v6

--- a/solution.py
+++ b/solution.py
@@ -453,7 +453,6 @@
         total = lax.fori_loop(0, chunks, residuals, jnp.zeros((1, WIDE), f32), unroll=True)
         v.e_src[it, 0:1] = total
         v.e_all[it, pl.ds(me, 1)] = total
-        v.r_all[it, r_rows] = v.r_src[it]
 
         @pl.when(it == 0)
         def _():
@@ -466,6 +465,8 @@
         to_partner(v.r_src.at[it], v.r_all.at[it, r_rows], v.r_sem.at[it])
         for mask in masks:
             remote(v.e_src.at[it, pl.ds(0, 1)], v.e_all.at[it, pl.ds(me, 1)], v.e_sem.at[it], peer_of(mask))
+
+        v.r_all[it, r_rows] = v.r_src[it]
 
         @pl.when(it == 0)
         def _():
@@ -477,17 +478,19 @@
             v.pairs_all[stn] = v.pairs[...]
             v.d_all[r_rows] = v.d_src[r_rows]
             wait_all(v.pairs_all.at[pl.ds(0, blocks - 1)], v.p_sem.at[1])
-            column = lax.broadcasted_iota(jnp.int32, (baselines, 128), 1).astype(f32)
+            column = lax.broadcasted_iota(jnp.int32, (baselines, 128), 1).astype(f32).astype(bf16)
             for i in range(blocks):
+                if i == blocks // 2:
+                    pass_on(it)
                 first = v.pairs_all[i, 0:1, :] & 127
                 second = v.pairs_all[i, 1:2, :]
                 v.index_p[i : i + 1, :] = first
                 v.index_q[i : i + 1, :] = second
                 for start, index in ((0, second & 127), (128, first)):
-                    across = jnp.broadcast_to(index.astype(f32), (128, baselines)).T
+                    across = jnp.broadcast_to(index.astype(f32).astype(bf16), (128, baselines)).T
                     v.collect[baselines * i : baselines * i + baselines, start : start + 128] = jnp.where(
-                        column == across, 1.0, 0.0
-                    ).astype(bf16)
+                        column == across, bf16(1.0), bf16(0.0)
+                    )
                 for j in range(tiles):
                     inside = jnp.where((second >> 7) == j, 1.0, 0.0)
                     at = 16 * (4 * i + j)
@@ -497,7 +500,6 @@
                 at = slice(WIDE * i, WIDE * i + WIDE)
                 for c in range(8):
                     v.d_own[8 * c : 8 * c + 8, at] = v.d_all[pl.ds(8 * i + c, blocks, stride=own_r), :]
-            pass_on(it)
             lax.fori_loop(0, chunks, own_terms, 0, unroll=True)
 
         @pl.when(it > 0)

time: 63.5 us -> 62.9 us (level)
  no operation moved by 1% of the time
where the time goes in v7:
time: 62.9 us; the launch traced here: 62.8 us
  Pallas kernels  62.1 us (99%)
  between operations  0.64 us (1%)
    pallas_call x1, Pallas kernels, body(): pl.pallas_call(run, out_shape=jax.ShapeDtypeStruct((32 * (2 + TERMS), 128...  61.4 us

profile of v7, /device:TPU:1, one launch (start us, length us, event | category | flops | bytes accessed | tf_op | source)
XLA Modules:
  0.0 62.8 jit_solution(499071871181432821)
XLA Ops:
  0.6 61.4 %calibrate.1.packed = f32[160,128]{1,0:T(8,128)S(1)} custom-call(s32[16]{0:T(128)} %bitcast.14, f32[8]{0:T(128)} %refs_1_.1, f32[8,1024]{1,0:T(8,128)} %bitcast.13, f32[128,1024]{1,0:T(8,128)} %bitcast.9, s32[2,1024]{1,0:T(2,128)} %refs_4_.1, f32[64,512]{1,0:T(8,128)} %bitcast.11, f32[192,512]{1,0:T(8,128)} %bitcast.10, f32[64,512]{1,0:T(8,128)} %bitcast.12), custom_call_target="tpu_custom_call" | custom-call | tf_op jit(solution)/shard_map/calibrate/pallas_call | solution.py:685
  62.0 0.7 %unpack.1 = (f32[64,64]{1,0:T(8,128)}, f32[64,64]{1,0:T(8,128)}, f32[192,64]{1,0:T(8,128)}) custom-call(f32[160,128]{1,0:T(8,128)S(1)} %calibrate.1.packed), custom_call_target="tpu_custom_call" | custom-call | tf_op jit(solution)/shard_map/unpack/pallas_call | solution.py:705

commit v8 on v7

--- a/solution.py
+++ b/solution.py
@@ -165,7 +165,7 @@
         ("p_sem", 2),
         ("d_sem", 2),
         ("e_sem", PASSES, 2),
-        ("r_sem", PASSES, 3),
+        ("r_sem", PASSES, 4),
         ("g_sem", PASSES, 2),
         ("f_sem", 2),
         ("s_sem", 2),
@@ -259,7 +259,7 @@
             src_ref=src,
             dst_ref=dst,
             send_sem=sem.at[0],
-            recv_sem=sem.at[2],
+            recv_sem=sem.at[3],
             device_id=peer_of(1),
             device_id_type=LOGICAL,
         ).start()
@@ -406,28 +406,35 @@
     own_g, own_r = stations // 16, baselines // 16
     g_rows = pl.ds(pl.multiple_of(own_g * stn, own_g), own_g)
     r_rows = pl.ds(pl.multiple_of(own_r * stn, own_r), own_r)
+    half = own_r // 2
+
+    def half_rows(block, part):
+        return pl.ds(pl.multiple_of(own_r * block + half * part, half), half)
+
+    even_masks = [mask for mask in stn_masks if mask % 2 == 0]
+
+    def send_residuals(it, part):
+        src = v.r_src.at[it, pl.ds(half * part, half)]
+        dst = v.r_all.at[it, half_rows(stn, part)]
+        for mask in even_masks:
+            pltpu.make_async_remote_copy(
+                src_ref=src,
+                dst_ref=dst,
+                send_sem=v.r_sem.at[it, 0],
+                recv_sem=v.r_sem.at[it, 1 + part],
+                device_id=peer_of(mask),
+                device_id_type=LOGICAL,
+            ).start()
+        to_partner(src, dst, v.r_sem.at[it])
 
     def pass_on(it):
-        wait_all(v.r_all.at[it, pl.ds(0, (blocks // 2 - 1) * own_r)], v.r_sem.at[it, 1])
-        for mask in stn_masks:
-            if mask % 2 == 0:
-                start = pl.multiple_of(own_r * (stn + lowers[mask]), own_r)
-                rows = v.r_all.at[it, pl.ds(start, own_r)]
+        for part in range(2):
+            wait_all(v.r_all.at[it, pl.ds(0, (blocks // 2 - 1) * half)], v.r_sem.at[it, 1 + part])
+            for mask in even_masks:
+                rows = v.r_all.at[it, half_rows(stn + lowers[mask], part)]
                 to_partner(rows, rows, v.r_sem.at[it])
 
-    def one_pass(it, _):
-        spread_tables()
-
-        @pl.when(it > 0)
-        def _():
-            lax.fori_loop(0, chunks, own_terms, 0, unroll=True)
-            wait_all(v.g_all.at[it - 1, pl.ds(0, (blocks - 1) * own_g)], v.g_sem.at[it - 1, 1])
-            for j in range(tiles):
-                for c in range(8):
-                    v.whole[64 * j + 8 * c : 64 * j + 8 * c + 8] = v.g_all[
-                        it - 1, pl.ds(8 * j + c, blocks, stride=own_g), :
-                    ]
-
+    def residuals_of(it, part):
         def residuals(i, total):
             at = chunk(i)
             first = jnp.broadcast_to(v.pairs[0:1, at], (8, WIDE)) & 127
@@ -450,19 +457,38 @@
                     v.r_src[it, pl.ds(8 * i + c, 1)] = left
             return total + e
 
-        total = lax.fori_loop(0, chunks, residuals, jnp.zeros((1, WIDE), f32), unroll=True)
+        first = part * chunks // 2
+        zero = jnp.zeros((1, WIDE), f32)
+        return lax.fori_loop(first, first + chunks // 2, residuals, zero, unroll=True)
+
+    def keep_energy(it, total):
         v.e_src[it, 0:1] = total
         v.e_all[it, pl.ds(me, 1)] = total
 
+    keep_energy(0, residuals_of(0, 0) + residuals_of(0, 1))
+    pl.semaphore_wait(barrier, everyone - 1)
+
+    def one_pass(it, _):
+        @pl.when(it > 0)
+        def _():
+            spread_tables()
+            lax.fori_loop(0, chunks, own_terms, 0, unroll=True)
+            wait_all(v.g_all.at[it - 1, pl.ds(0, (blocks - 1) * own_g)], v.g_sem.at[it - 1, 1])
+            for j in range(tiles):
+                for c in range(8):
+                    v.whole[64 * j + 8 * c : 64 * j + 8 * c + 8] = v.g_all[
+                        it - 1, pl.ds(8 * j + c, blocks, stride=own_g), :
+                    ]
+            total = residuals_of(it, 0)
+            send_residuals(it, 0)
+            keep_energy(it, total + residuals_of(it, 1))
+
         @pl.when(it == 0)
         def _():
-            pl.semaphore_wait(barrier, everyone - 1)
             to_stn(lambda _: v.pairs, v.pairs_all.at[stn], v.p_sem)
-
-        for mask in stn_masks:
-            if mask % 2 == 0:
-                remote(v.r_src.at[it], v.r_all.at[it, r_rows], v.r_sem.at[it], peer_of(mask))
-        to_partner(v.r_src.at[it], v.r_all.at[it, r_rows], v.r_sem.at[it])
+            send_residuals(it, 0)
+
+        send_residuals(it, 1)
         for mask in masks:
             remote(v.e_src.at[it, pl.ds(0, 1)], v.e_all.at[it, pl.ds(me, 1)], v.e_sem.at[it], peer_of(mask))
 
@@ -475,6 +501,7 @@
                 v.d_all.at[r_rows],
                 v.d_sem,
             )
+            spread_tables()
             v.pairs_all[stn] = v.pairs[...]
             v.d_all[r_rows] = v.d_src[r_rows]
             wait_all(v.pairs_all.at[pl.ds(0, blocks - 1)], v.p_sem.at[1])
@@ -506,7 +533,7 @@
         def _():
             pass_on(it)
 
-        wait_all(v.r_all.at[it, pl.ds(0, blocks // 2 * own_r)], v.r_sem.at[it, 2])
+        wait_all(v.r_all.at[it, pl.ds(0, blocks // 2 * own_r)], v.r_sem.at[it, 3])
 
         def products(i, _):
             at = chunk(i)

time: 62.9 us -> 62.6 us (level)
  no operation moved by 1% of the time
where the time goes in v8:
time: 62.6 us; the launch traced here: 62.5 us
  Pallas kernels  61.9 us (99%)
  between operations  0.64 us (1%)
    pallas_call x1, Pallas kernels, body(): pl.pallas_call(run, out_shape=jax.ShapeDtypeStruct((32 * (2 + TERMS), 128...  61.1 us

profile of v8, /device:TPU:1, one launch (start us, length us, event | category | flops | bytes accessed | tf_op | source)
XLA Modules:
  0.0 62.5 jit_solution(17722578725413572208)
XLA Ops:
  0.6 61.1 %calibrate.1.packed = f32[160,128]{1,0:T(8,128)S(1)} custom-call(s32[16]{0:T(128)} %bitcast.14, f32[8]{0:T(128)} %refs_1_.1, f32[8,1024]{1,0:T(8,128)} %bitcast.13, f32[128,1024]{1,0:T(8,128)} %bitcast.9, s32[2,1024]{1,0:T(2,128)} %refs_4_.1, f32[64,512]{1,0:T(8,128)} %bitcast.11, f32[192,512]{1,0:T(8,128)} %bitcast.10, f32[64,512]{1,0:T(8,128)} %bitcast.12), custom_call_target="tpu_custom_call" | custom-call | tf_op jit(solution)/shard_map/calibrate/pallas_call | solution.py:712
  61.8 0.7 %unpack.1 = (f32[64,64]{1,0:T(8,128)}, f32[64,64]{1,0:T(8,128)}, f32[192,64]{1,0:T(8,128)}) custom-call(f32[160,128]{1,0:T(8,128)S(1)} %calibrate.1.packed), custom_call_target="tpu_custom_call" | custom-call | tf_op jit(solution)/shard_map/unpack/pallas_call | solution.py:732

commit v9 on v8

--- a/solution.py
+++ b/solution.py
@@ -529,6 +529,18 @@
                     v.d_own[8 * c : 8 * c + 8, at] = v.d_all[pl.ds(8 * i + c, blocks, stride=own_r), :]
             lax.fori_loop(0, chunks, own_terms, 0, unroll=True)
 
+        @pl.when(it == INNER)
+        def _():
+            wait_all(v.f_all.at[pl.ds(0, chans - 1)], v.f_sem.at[1])
+            fit = [jnp.zeros((own_g, 128), f32)] * TERMS
+            for f in range(chans):
+                value = v.f_all[f]
+                fit = [fit[t] + f32(table[f, t]) * value for t in range(TERMS)]
+            consensus = consensus_of([z * f32(1.0 / chans) for z in fit])
+            after = v.f_src[...] - consensus
+            v.dual[...] = after
+            to_tiles(v.anchor, consensus - after)
+
         @pl.when(it > 0)
         def _():
             pass_on(it)
@@ -550,18 +562,6 @@
             return 0
 
         lax.fori_loop(0, chunks, products, 0, unroll=True)
-
-        @pl.when(it == INNER)
-        def _():
-            wait_all(v.f_all.at[pl.ds(0, chans - 1)], v.f_sem.at[1])
-            fit = [jnp.zeros((own_g, 128), f32)] * TERMS
-            for f in range(chans):
-                value = v.f_all[f]
-                fit = [fit[t] + f32(table[f, t]) * value for t in range(TERMS)]
-            consensus = consensus_of([z * f32(1.0 / chans) for z in fit])
-            after = v.f_src[...] - consensus
-            v.dual[...] = after
-            to_tiles(v.anchor, consensus - after)
 
         wait_all(v.e_all.at[it, pl.ds(0, everyone - 1)], v.e_sem.at[it, 1])
         total = jnp.sum(v.e_all[it], axis=0, keepdims=True)
@@ -660,6 +660,14 @@
     to_stn(lambda peer: v.j_src.at[peer], v.j_all.at[stn], v.j_sem)
     v.s_all[me] = v.s_src[stn]
     v.j_all[stn] = v.j_src[stn]
+    wait_all(v.pairs_all.at[pl.ds(0, blocks - 1)], v.p_sem.at[0])
+    wait_all(v.d_all.at[pl.ds(0, (blocks - 1) * own_r)], v.d_sem.at[0])
+    wait_all(v.f_all.at[pl.ds(0, chans - 1)], v.f_sem.at[0])
+    for it in range(PASSES):
+        wait_all(v.e_all.at[it, pl.ds(0, everyone - 1)], v.e_sem.at[it, 0])
+        wait_all(v.r_all.at[it, pl.ds(0, (blocks - 1) * own_r)], v.r_sem.at[it, 0])
+        if it < PASSES - 1:
+            wait_all(v.g_all.at[it, pl.ds(0, (blocks - 1) * own_g)], v.g_sem.at[it, 0])
     wait_all(v.j_all.at[pl.ds(0, blocks - 1)], v.j_sem.at[1])
 
     packed[0:32, :] = v.j_all[...].reshape(32, 128)
@@ -673,16 +681,8 @@
     for t in range(TERMS):
         packed[64 + 32 * t : 96 + 32 * t, :] = fit[t]
 
-    wait_all(v.pairs_all.at[pl.ds(0, blocks - 1)], v.p_sem.at[0])
-    wait_all(v.d_all.at[pl.ds(0, (blocks - 1) * own_r)], v.d_sem.at[0])
-    wait_all(v.f_all.at[pl.ds(0, chans - 1)], v.f_sem.at[0])
     wait_all(v.s_all.at[pl.ds(0, everyone - 1)], v.s_sem.at[0])
     wait_all(v.j_all.at[pl.ds(0, blocks - 1)], v.j_sem.at[0])
-    for it in range(PASSES):
-        wait_all(v.e_all.at[it, pl.ds(0, everyone - 1)], v.e_sem.at[it, 0])
-        wait_all(v.r_all.at[it, pl.ds(0, (blocks - 1) * own_r)], v.r_sem.at[it, 0])
-        if it < PASSES - 1:
-            wait_all(v.g_all.at[it, pl.ds(0, (blocks - 1) * own_g)], v.g_sem.at[it, 0])
 
 
 def unpack(packed, gain_out, dual_out, fit_out):

time: 62.6 us -> 62.6 us (level)
  no operation moved by 1% of the time
where the time goes in v9:
time: 62.6 us; the launch traced here: 62.5 us
  Pallas kernels  61.9 us (99%)
  between operations  0.64 us (1%)
    pallas_call x1, Pallas kernels, body(): pl.pallas_call(run, out_shape=jax.ShapeDtypeStruct((32 * (2 + TERMS), 128...  61.1 us

profile of v9, /device:TPU:1, one launch (start us, length us, event | category | flops | bytes accessed | tf_op | source)
XLA Modules:
  0.0 62.5 jit_solution(13984435608423051915)
XLA Ops:
  0.6 61.1 %calibrate.1.packed = f32[160,128]{1,0:T(8,128)S(1)} custom-call(s32[16]{0:T(128)} %bitcast.14, f32[8]{0:T(128)} %refs_1_.1, f32[8,1024]{1,0:T(8,128)} %bitcast.13, f32[128,1024]{1,0:T(8,128)} %bitcast.9, s32[2,1024]{1,0:T(2,128)} %refs_4_.1, f32[64,512]{1,0:T(8,128)} %bitcast.11, f32[192,512]{1,0:T(8,128)} %bitcast.10, f32[64,512]{1,0:T(8,128)} %bitcast.12), custom_call_target="tpu_custom_call" | custom-call | tf_op jit(solution)/shard_map/calibrate/pallas_call | solution.py:712
  61.8 0.7 %unpack.1 = (f32[64,64]{1,0:T(8,128)}, f32[64,64]{1,0:T(8,128)}, f32[192,64]{1,0:T(8,128)}) custom-call(f32[160,128]{1,0:T(8,128)S(1)} %calibrate.1.packed), custom_call_target="tpu_custom_call" | custom-call | tf_op jit(solution)/shard_map/unpack/pallas_call | solution.py:732
